TPU v7x, 32 devices: a whole 2x2x4 slice. The times are simulated.
32 devices in a mesh: group: 1, wide: 32 (over z, y, x, core).
Axes of the slice: x: 2, y: 2, z: 4, core: 2. Of those that a mesh axis runs over, the one named last changes fastest.
Arguments:
- resid: bfloat16 [32, 3072], P(('group', 'wide')), may hold values from -6 to 6
- query: bfloat16 [32, 4096], P(('group', 'wide')), may hold values from -4 to 4
- key: bfloat16 [32, 4096], P(('group', 'wide')), may hold values from -4 to 4
- value: bfloat16 [32, 4096], P(('group', 'wide')), may hold values from -6 to 6
- state: float32 [32, 32, 128, 128], P(('group', 'wide')), may hold values from -6 to 6
- decay: float32 [32], replicated, may hold values from 0.02 to 2
- out_gate: bfloat16 [32, 4096], P(('group', 'wide')), may hold values from -6 to 6
- norm_gain: float32 [4096], replicated, may hold values from 0.25 to 1.75
- w_out: bfloat16 [4096, 3072], P('wide'), may hold values from -0.09375 to 0.09375
- moe_gain: float32 [3072], replicated, may hold values from 0.25 to 1.75
- w_gate: bfloat16 [32, 576, 3072], P('wide'), may hold values from -0.109375 to 0.109375
- w_up: bfloat16 [32, 576, 3072], P('wide'), may hold values from -0.109375 to 0.109375
- w_down: bfloat16 [32, 576, 3072], P('wide'), may hold values from -0.09375 to 0.09375
- expert_ids: int32 [32, 2], P('group'), may hold values from 0 to 3, all different within a row; in each aligned block of 32 rows (0 to 31, 32 to 63, ...) at most 32 rows name the same one
- expert_weights: float32 [32, 2], P('group'), may hold values from 0.2 to 1
Outputs:
- mixed: bfloat16 [32, 3072], P(('group', 'wide'))
Inputs may be any that keep to these rules, and one draw needn't show every extreme that they name: `expert_ids`: each request names two different experts; every expert is named by some request; no expert is named by more than 32 requests, a bound that some block reaches.
All inputs are finite; a program needn't handle non-finite values.
Results may differ from a plain program's by a relative error of at most 0.012.
Values may be sent and summed in bfloat16 or wider, within the bound.
No kernel may reach another device: no remote copies, remote signals or barrier semaphores. Data moves between devices by JAX's collectives and lax.ppermute only.
A program may use at most 64 MiB of HBM per device.

v0:
```python
import jax
import jax.numpy as jnp
from jax import lax
from jax.sharding import PartitionSpec as P

SPLIT = 8


def by_rows(left, weight):
    return lax.dot_general(
        left, weight, (((1,), (1,)), ((), ())), preferred_element_type=jnp.float32
    )


def shards(
    resid,
    query,
    key,
    value,
    state,
    decay,
    out_gate,
    norm_gain,
    w_out,
    moe_gain,
    w_gate,
    w_up,
    w_down,
    expert_ids,
    expert_weights,
):
    local_rows = resid.shape[0]
    heads = decay.shape[0]
    head_size = query.shape[1] // heads
    devices = lax.axis_size("wide")
    q_heads = query.astype(jnp.float32).reshape(local_rows, heads, head_size)
    k_heads = key.astype(jnp.float32).reshape(local_rows, heads, head_size)
    v_heads = value.astype(jnp.float32).reshape(local_rows, heads, head_size)
    fade = jnp.exp(-decay)
    new_state = fade[None, :, None, None] * state + jnp.einsum("rhi,rhj->rhij", k_heads, v_heads)
    att = jnp.einsum("rhi,rhij->rhj", q_heads, new_state).reshape(local_rows, heads * head_size)
    scale = lax.rsqrt(jnp.mean(att * att, axis=1, keepdims=True) + 1e-06)
    attn = (att * scale * norm_gain * jax.nn.sigmoid(out_gate.astype(jnp.float32))).astype(
        jnp.bfloat16
    )
    columns = lax.all_to_all(attn, "wide", split_axis=1, concat_axis=0, tiled=True)
    piece = columns
    proj = lax.psum_scatter(
        jnp.dot(piece, w_out, preferred_element_type=jnp.float32),
        "wide",
        scatter_dimension=0,
        tiled=True,
    )
    hid_res = (resid.astype(jnp.float32) + proj).astype(jnp.bfloat16)
    hid_f = hid_res.astype(jnp.float32)
    normed = (
        hid_f * lax.rsqrt(jnp.mean(hid_f * hid_f, axis=1, keepdims=True) + 1e-06) * moe_gain
    ).astype(jnp.bfloat16)
    all_inputs = lax.all_gather(normed, "wide", axis=0, tiled=True)
    owner = lax.axis_index("wide") // SPLIT
    weight_all = jnp.sum(jnp.where(expert_ids == owner, expert_weights, 0.0), axis=1)
    piece = all_inputs
    gate = by_rows(piece, w_gate[0])
    upper = by_rows(piece, w_up[0])
    inner = (jax.nn.silu(gate) * upper).astype(jnp.bfloat16)
    partial_value = (
        jnp.dot(inner, w_down[0], preferred_element_type=jnp.float32) * weight_all[:, None]
    ).reshape(devices, local_rows, hid_f.shape[1])
    returned = lax.all_to_all(partial_value, "wide", split_axis=0, concat_axis=0, tiled=True)
    experts_out = jnp.sum(returned, axis=0)
    return (hid_f + experts_out).astype(jnp.bfloat16)


def solution(mesh):
    return jax.shard_map(
        shards,
        mesh=mesh,
        in_specs=(
            P(("group", "wide"), None),
            P(("group", "wide"), None),
            P(("group", "wide"), None),
            P(("group", "wide"), None),
            P(("group", "wide"), None, None, None),
            P(),
            P(("group", "wide"), None),
            P(),
            P("wide", None),
            P(),
            P("wide", None, None),
            P("wide", None, None),
            P("wide", None, None),
            P("group", None),
            P("group", None),
        ),
        out_specs=P(("group", "wide"), None),
        check_vma=False,
    )
```

profile of v0, /device:TPU:0, one launch (start us, length us, event | category | flops | bytes accessed | tf_op | source)
XLA Modules:
  0.0 235.7 jit_solution(16891972919051586054)
XLA Ops:
  6.5 0.0 copy-start
  6.5 0.0 all-reduce.3.cloned.1.call-start
  6.5 0.8 negate_exponential_fusion
  7.3 0.9 convert.12
  8.3 0.7 convert.13
  9.0 2.3 fusion.12
  11.3 0.6 multiply_reduce_fusion
  12.7 0.7 bitcast_multiply_fusion
  13.4 0.8 convert_bitcast_fusion
  14.1 14.3 %all_to_all.21 = bf16[1,32,128]{2,0,1:T(2,128)(2,1)S(1)} all-to-all(bf16[1,32,128]{2,0,1:T(2,128)(2,1)S(1)} %convert_bitcast_fusion), channel_id=1, replica_groups=mesh['group'=1,'wide'=32] {'wide'}, dimensions={1} | all-to-all | bytes 16384 | tf_op jit(solution)/shard_map/all_to_all | solution.py:46
  28.5 2.1 fusion.42
  30.6 0.0 all-reduce.3.cloned.1.call-update
  30.6 0.7 fusion.45
  31.3 124.6 %all-reduce.3.cloned.1.call-done = f32[32,3072]{1,0:T(8,128)} async-done(((f32[32,3072]{1,0:T(8,128)}), f32[32,3072]{1,0:T(8,128)}) %all-reduce.3.cloned.1.call-update) | async-done | bytes 393232
  156.0 1.5 multiply_reduce_fusion.1
  158.2 0.7 convert_bitcast_fusion.1
  158.9 40.6 %all-gather = bf16[32,1,3072]{2,1,0:T(2,128)(2,1)S(1)} all-gather(bf16[1,1,3072]{2,1,0:T(2,128)(2,1)S(1)} %convert_bitcast_fusion.1), channel_id=1, replica_groups=mesh['group'=1,'wide'=32] {'wide'}, dimensions={0}, use_global_device_ids=true | all-gather | bytes 202752 | tf_op jit(solution)/shard_map/all_gather | solution.py:59
  199.5 0.0 copy-start.1
  199.5 0.7 copy-done.1
  200.3 3.8 %fusion.4 = f32[32,576]{1,0:T(8,128)} fusion(bf16[1,576,3072]{2,1,0:T(8,128)(2,1)} %param.25, bf16[32,1,3072]{2,1,0:T(2,128)(2,1)S(1)} %all-gather), kind=kOutput, calls=%fused_computation.4 | convolution fusion | flops 113246208 | bytes 3809280 | tf_op jit(solution)/shard_map/dot_general | solution.py:10
  204.0 0.0 copy-done
  204.0 4.7 %fusion.9 = f32[32,1,3072]{2,0,1:T(8,128)} fusion(bf16[1,576,3072]{2,1,0:T(8,128)(2,1)S(1)} %copy-done, bf16[1,576,3072]{2,1,0:T(8,128)(2,1)} %param.26, f32[32]{0:T(128)S(1)} %fusion.45, f32[32,576]{1,0:T(8,128)} %fusion.4, bf16[32,1,3072]{2,1,0:T(2,128)(2,1)} %copy-done.1), kind=kOutput, calls=%fused_computation.7 | convolution fusion | flops 226701312 | bytes 7741568 | tf_op jit(solution)/shard_map/dot_general | solution.py:67
  208.7 1.4 copy.18
  210.1 15.6 %all_to_all.22 = f32[32,1,3072]{2,1,0:T(1,128)} all-to-all(f32[32,1,3072]{2,1,0:T(1,128)S(1)} %copy.18), channel_id=1, replica_groups=mesh['group'=1,'wide'=32] {'wide'}, dimensions={0} | all-to-all | bytes 786432 | tf_op jit(solution)/shard_map/all_to_all | solution.py:69
  225.7 1.8 reduce_sum.41
  227.6 1.3 add_convert_fusion
Async XLA Ops:
  6.5 197.5 %copy-start = (bf16[1,576,3072]{2,1,0:T(8,128)(2,1)S(1)}, bf16[1,576,3072]{2,1,0:T(8,128)(2,1)}, u32[]{:S(2)}) copy-start(bf16[1,576,3072]{2,1,0:T(8,128)(2,1)} %param.27) | copy-start | bytes 10616836
  6.5 149.4 %all-reduce.3.cloned.1.call-start = ((), (), s32[]{:S(2)}) async-start(), calls=%async_computation.2 | async-start | bytes 786432
  199.5 0.7 copy-start.1
Sparse Core Ops, SparseCore 0:
  30.7 125.1 all-reduce.2
where the time goes:
time: 237 us; the launch traced here: 236 us
  waiting for transfers between devices  125 us (53%)
  blocking collectives  70.6 us (30%)
  between operations  14.8 us (6%)
  matrix products  12.9 us (5%)
  other arithmetic  10.7 us (5%)
    unnamed x2, waiting for transfers between devices  125 us
    all_gather x1, blocking collectives, shards(): all_inputs = lax.all_gather(normed, 'wide', axis=0, tiled=True)  40.6 us
    all_to_all x1, blocking collectives, shards(): lax.all_to_all(partial_value, 'wide', split_axis=0, concat_axis=0, tiled=...  15.6 us
    all_to_all x1, blocking collectives, shards(): lax.all_to_all(attn, 'wide', split_axis=1, concat_axis=0, tiled=True)  14.3 us
  transfers between devices with their start and end apart: 1, of which 1 were waited for; matrix products, arithmetic and copies ran while one was open for 0% of the time, Pallas kernels for 0%

commit v1 on v0

--- a/solution.py
+++ b/solution.py
@@ -10,6 +10,10 @@
     return lax.dot_general(
         left, weight, (((1,), (1,)), ((), ())), preferred_element_type=jnp.float32
     )
+
+
+def exchange(blocks):
+    return lax.all_to_all(blocks, "wide", split_axis=0, concat_axis=0, tiled=True)
 
 
 def shards(
@@ -29,10 +33,11 @@
     expert_ids,
     expert_weights,
 ):
-    local_rows = resid.shape[0]
+    local_rows, width = resid.shape
     heads = decay.shape[0]
     head_size = query.shape[1] // heads
     devices = lax.axis_size("wide")
+    rows = devices * local_rows
     q_heads = query.astype(jnp.float32).reshape(local_rows, heads, head_size)
     k_heads = key.astype(jnp.float32).reshape(local_rows, heads, head_size)
     v_heads = value.astype(jnp.float32).reshape(local_rows, heads, head_size)
@@ -44,30 +49,25 @@
         jnp.bfloat16
     )
     columns = lax.all_to_all(attn, "wide", split_axis=1, concat_axis=0, tiled=True)
-    piece = columns
-    proj = lax.psum_scatter(
-        jnp.dot(piece, w_out, preferred_element_type=jnp.float32),
-        "wide",
-        scatter_dimension=0,
-        tiled=True,
-    )
-    hid_res = (resid.astype(jnp.float32) + proj).astype(jnp.bfloat16)
+    proj = jnp.dot(columns, w_out, preferred_element_type=jnp.float32).astype(jnp.bfloat16)
+    parts = exchange(proj.reshape(devices, local_rows, width))
+    summed = jnp.sum(parts.astype(jnp.float32), axis=0)
+    hid_res = (resid.astype(jnp.float32) + summed).astype(jnp.bfloat16)
     hid_f = hid_res.astype(jnp.float32)
     normed = (
         hid_f * lax.rsqrt(jnp.mean(hid_f * hid_f, axis=1, keepdims=True) + 1e-06) * moe_gain
     ).astype(jnp.bfloat16)
-    all_inputs = lax.all_gather(normed, "wide", axis=0, tiled=True)
+    all_inputs = exchange(jnp.broadcast_to(normed[None], (devices, local_rows, width)))
+    all_inputs = all_inputs.reshape(rows, width)
     owner = lax.axis_index("wide") // SPLIT
     weight_all = jnp.sum(jnp.where(expert_ids == owner, expert_weights, 0.0), axis=1)
-    piece = all_inputs
-    gate = by_rows(piece, w_gate[0])
-    upper = by_rows(piece, w_up[0])
+    gate = by_rows(all_inputs, w_gate[0])
+    upper = by_rows(all_inputs, w_up[0])
     inner = (jax.nn.silu(gate) * upper).astype(jnp.bfloat16)
-    partial_value = (
-        jnp.dot(inner, w_down[0], preferred_element_type=jnp.float32) * weight_all[:, None]
-    ).reshape(devices, local_rows, hid_f.shape[1])
-    returned = lax.all_to_all(partial_value, "wide", split_axis=0, concat_axis=0, tiled=True)
-    experts_out = jnp.sum(returned, axis=0)
+    partial_value = jnp.dot(inner, w_down[0], preferred_element_type=jnp.float32)
+    partial_value = (partial_value * weight_all[:, None]).astype(jnp.bfloat16)
+    returned = exchange(partial_value.reshape(devices, local_rows, width))
+    experts_out = jnp.sum(returned.astype(jnp.float32), axis=0)
     return (hid_f + experts_out).astype(jnp.bfloat16)
 
 

time: 237 us -> 98.7 us (0.42)
  waiting for transfers between devices: 125 us -> 8.21 us
  blocking collectives: 70.6 us -> 38.7 us
  between operations: 14.8 us -> 1.48 us
  local copies, waits for them, and re-layouts: 2.14 us -> 13.4 us
  other arithmetic: 10.7 us -> 19.5 us
  starting transfers between devices: 0.01 us -> 3.28 us
    unnamed x2 -> x0, waiting for transfers between devices: 125 us -> none
    all_gather x1 -> x0, blocking collectives: 40.6 us -> none  [shards(): all_inputs = lax.all_gather(normed, 'wide', axis=0, tiled=True)]
    unnamed x4 -> x8, local copies, waits for them, and re-layouts: 0.74 us -> 11.9 us
    all_to_all x1 -> x2, blocking collectives: 15.6 us -> 24.4 us  [exchange(): lax.all_to_all(blocks, 'wide', split_axis=0, concat_axis=0, tiled=True)]
    all_to_all x0 -> x1, waiting for transfers between devices: none -> 8.21 us  [exchange(): lax.all_to_all(blocks, 'wide', split_axis=0, concat_axis=0, tiled=True)]
    reshape x0 -> x2, other arithmetic: none -> 4.65 us  [the longest x1 2.32 us: shards(): parts = exchange(proj.reshape(devices, local_rows, width))]
    broadcast_in_dim x0 -> x1, other arithmetic: none -> 3.39 us  [shards(): jnp.broadcast_to(normed[None], (devices, local_rows, width))]
    all_to_all x0 -> x1, starting transfers between devices: none -> 3.28 us  [exchange(): lax.all_to_all(blocks, 'wide', split_axis=0, concat_axis=0, tiled=True)]
  transfers between devices with their start and end apart: 1 -> 1, of which waited for: 1 -> 1; matrix products, arithmetic and copies ran while one was open for 0% -> 1% of each run, Pallas kernels for 0% -> 0%
where the time goes in v1:
time: 98.7 us; the launch traced here: 97.5 us
  blocking collectives  38.7 us (39%)
  other arithmetic  19.5 us (20%)
  local copies, waits for them, and re-layouts  13.4 us (14%)
  matrix products  12.9 us (13%)
  waiting for transfers between devices  8.21 us (8%)
  starting transfers between devices  3.28 us (3%)
  between operations  1.48 us (1%)
    all_to_all x2, blocking collectives, exchange(): lax.all_to_all(blocks, 'wide', split_axis=0, concat_axis=0, tiled=True)  24.4 us
    all_to_all x1, blocking collectives, shards(): lax.all_to_all(attn, 'wide', split_axis=1, concat_axis=0, tiled=True)  14.3 us
    unnamed x8, local copies, waits for them, and re-layouts  11.9 us
    all_to_all x1, waiting for transfers between devices, exchange(): lax.all_to_all(blocks, 'wide', split_axis=0, concat_axis=0, tiled=True)  8.21 us
    dot_general x1, matrix products, shards(): jnp.dot(inner, w_down[0], preferred_element_type=jnp.float32)  4.59 us
    dot_general x1, matrix products, by_rows(): lax.dot_general(left, weight, (((1,), (1,)), ((), ())), preferred_element...  3.91 us
    broadcast_in_dim x1, other arithmetic, shards(): jnp.broadcast_to(normed[None], (devices, local_rows, width))  3.39 us
    all_to_all x1, starting transfers between devices, exchange(): lax.all_to_all(blocks, 'wide', split_axis=0, concat_axis=0, tiled=True)  3.28 us
  transfers between devices with their start and end apart: 1, of which 1 were waited for; matrix products, arithmetic and copies ran while one was open for 1% of the time, Pallas kernels for 0%

profile of v1, /device:TPU:0, one launch (start us, length us, event | category | flops | bytes accessed | tf_op | source)
XLA Modules:
  0.0 97.5 jit_solution(9340991607420980988)
XLA Ops:
  0.0 0.0 copy-start
  0.0 0.8 negate_exponential_fusion
  0.8 0.9 convert.12
  1.7 0.7 convert.13
  2.5 2.3 %fusion.16 = f32[32,1,128]{2,1,0:T(1,128)S(1)} fusion(f32[1,32,128,128]{3,2,1,0:T(8,128)} %param.19, f32[32,128]{1,0:T(8,128)S(1)} %bitcast.64, f32[32,128]{1,0:T(8,128)S(1)} %bitcast.63, f32[32]{0:T(128)S(1)} %negate_exponential_fusion, bf16[1,4096]{1,0:T(2,128)(2,1)} %param.16), kind=kOutput, calls=%fused_computation.11 | convolution fusion | flops 2621440 | bytes 2154624 | tf_op jit(solution)/shard_map/rhi,rhij->rhj/dot_general | solution.py:46
  4.8 0.6 multiply_reduce_fusion
  6.1 0.7 bitcast_multiply_fusion
  6.8 0.8 convert_bitcast_fusion
  7.6 14.3 %all_to_all.31 = bf16[1,32,128]{2,0,1:T(2,128)(2,1)S(1)} all-to-all(bf16[1,32,128]{2,0,1:T(2,128)(2,1)S(1)} %convert_bitcast_fusion), channel_id=1, replica_groups=mesh['group'=1,'wide'=32] {'wide'}, dimensions={1} | all-to-all | bytes 16384 | tf_op jit(solution)/shard_map/all_to_all | solution.py:51
  21.9 2.1 %fusion.15 = bf16[32,1,3072]{2,0,1:T(8,128)(2,1)} fusion(bf16[128,3072]{1,0:T(8,128)(2,1)} %param.23, bf16[1,32,128]{2,0,1:T(2,128)(2,1)S(1)} %all_to_all.31), kind=kOutput, calls=%fused_computation.10 | convolution fusion | flops 25264128 | bytes 991232 | tf_op jit(solution)/shard_map/dot_general | solution.py:52
  24.0 0.5 broadcast.22
  24.5 2.3 %reduce.6 = bf16[32,3072]{1,0:T(8,128)(2,1)} reduce(bf16[32,1,3072]{2,0,1:T(8,128)(2,1)} %fusion.15, bf16[]{:T(256)} %broadcast.22), dimensions={1}, to_apply=%copy.20.reduce_sub_computation | reduce | bytes 393218 | tf_op jit(solution)/shard_map/reshape | solution.py:53
  26.8 1.7 %reshape.91 = bf16[32,2,1536]{2,1,0:T(2,128)(2,1)} reshape(bf16[32,3072]{1,0:T(8,128)(2,1)} %reduce.6) | data formatting | bytes 393216
  28.6 12.2 %all_to_all.32 = bf16[32,2,1536]{2,1,0:T(2,128)(2,1)} all-to-all(bf16[32,2,1536]{2,1,0:T(2,128)(2,1)} %reshape.91), channel_id=1, replica_groups=mesh['group'=1,'wide'=32] {'wide'}, dimensions={0} | all-to-all | bytes 393216 | tf_op jit(solution)/shard_map/all_to_all | solution.py:16
  40.8 2.2 %reshape.92 = bf16[32,1,3072]{2,1,0:T(2,128)(2,1)} reshape(bf16[32,2,1536]{2,1,0:T(2,128)(2,1)} %all_to_all.32) | data formatting | bytes 393216
  43.0 1.4 %convert_reduce_fusion.1 = f32[3072]{0:T(1024)S(1)} fusion(bf16[32,1,3072]{2,1,0:T(2,128)(2,1)} %reshape.92), kind=kLoop, calls=%fused_computation.22 | loop fusion | flops 193536 | bytes 208896 | tf_op jit(solution)/shard_map/reduce_sum | solution.py:54
  44.4 1.4 %multiply_reduce_fusion.1 = f32[]{:T(128)} fusion(f32[1,3072]{1,0:T(1,128)S(1)} %bitcast.58, bf16[1,3072]{1,0:T(2,128)(2,1)} %param.15), kind=kLoop, calls=%fused_computation.40 | loop fusion | flops 18431 | bytes 18436 | tf_op jit(solution)/shard_map/reduce_sum | solution.py:58
  46.5 0.8 convert_reduce_fusion.2
  47.3 0.9 broadcast_in_dim.22
  48.2 3.4 %reduce.7 = bf16[32,3072]{1,0:T(8,128)(2,1)} reduce(bf16[32,1,3072]{2,1,0:T(2,128)(2,1)} %broadcast_in_dim.22, bf16[]{:T(256)} %broadcast.22), dimensions={1}, to_apply=%broadcast_in_dim.22.reduce_sub_computation | reduce | bytes 393218 | tf_op jit(solution)/shard_map/broadcast_in_dim | solution.py:60
  51.6 1.7 %reshape.93 = bf16[32,2,1536]{2,1,0:T(2,128)(2,1)} reshape(bf16[32,3072]{1,0:T(8,128)(2,1)} %reduce.7) | data formatting | bytes 393216
  53.4 3.3 %all-to-all-start.2 = ((bf16[32,2,1536]{2,1,0:T(2,128)(2,1)}), bf16[32,2,1536]{2,1,0:T(2,128)(2,1)}, u32[]{:S(2)}, u32[]{:S(2)}) async-start(bf16[32,2,1536]{2,1,0:T(2,128)(2,1)} %reshape.93), calls=%async_computation.2 | async-start | bytes 393216 | tf_op jit(solution)/shard_map/all_to_all | solution.py:16
  56.7 0.7 fusion.46
  57.4 8.2 %all-to-all-done.2 = bf16[32,2,1536]{2,1,0:T(2,128)(2,1)} async-done(((bf16[32,2,1536]{2,1,0:T(2,128)(2,1)}), bf16[32,2,1536]{2,1,0:T(2,128)(2,1)}, u32[]{:S(2)}, u32[]{:S(2)}) %all-to-all-start.2) | async-done | bytes 196640 | tf_op jit(solution)/shard_map/all_to_all | solution.py:16
  65.6 2.2 %reshape.94 = bf16[32,1,3072]{2,1,0:T(2,128)(2,1)} reshape(bf16[32,2,1536]{2,1,0:T(2,128)(2,1)} %all-to-all-done.2) | data formatting | bytes 393216
  67.8 3.9 %fusion.4 = f32[32,576]{1,0:T(8,128)} fusion(bf16[1,576,3072]{2,1,0:T(8,128)(2,1)} %param.25, bf16[32,1,3072]{2,1,0:T(2,128)(2,1)} %reshape.94), kind=kOutput, calls=%fused_computation.4 | convolution fusion | flops 113246208 | bytes 3809280 | tf_op jit(solution)/shard_map/dot_general | solution.py:10
  71.7 0.0 copy-done
  71.7 4.6 %fusion.12 = bf16[32,1,3072]{2,0,1:T(8,128)(2,1)} fusion(bf16[1,576,3072]{2,1,0:T(8,128)(2,1)S(1)} %copy-done, bf16[1,576,3072]{2,1,0:T(8,128)(2,1)} %param.26, f32[32]{0:T(128)S(1)} %fusion.46, f32[32,576]{1,0:T(8,128)} %fusion.4, bf16[32,1,3072]{2,1,0:T(2,128)(2,1)} %reshape.94), kind=kOutput, calls=%fused_computation.9 | convolution fusion | flops 226799616 | bytes 7544960 | tf_op jit(solution)/shard_map/dot_general | solution.py:67
  76.3 2.3 %reduce.8 = bf16[32,3072]{1,0:T(8,128)(2,1)} reduce(bf16[32,1,3072]{2,0,1:T(8,128)(2,1)} %fusion.12, bf16[]{:T(256)} %broadcast.22), dimensions={1}, to_apply=%copy.21.reduce_sub_computation | reduce | bytes 393218 | tf_op jit(solution)/shard_map/reshape | solution.py:69
  78.7 1.7 %reshape.95 = bf16[32,2,1536]{2,1,0:T(2,128)(2,1)} reshape(bf16[32,3072]{1,0:T(8,128)(2,1)} %reduce.8) | data formatting | bytes 393216
  80.4 12.2 %all_to_all.33 = bf16[32,2,1536]{2,1,0:T(2,128)(2,1)} all-to-all(bf16[32,2,1536]{2,1,0:T(2,128)(2,1)} %reshape.95), channel_id=1, replica_groups=mesh['group'=1,'wide'=32] {'wide'}, dimensions={0} | all-to-all | bytes 393216 | tf_op jit(solution)/shard_map/all_to_all | solution.py:16
  92.6 2.2 %reshape.96 = bf16[32,1,3072]{2,1,0:T(2,128)(2,1)} reshape(bf16[32,2,1536]{2,1,0:T(2,128)(2,1)} %all_to_all.33) | data formatting | bytes 393216
  94.8 1.4 %convert_reduce_fusion = f32[3072]{0:T(1024)S(1)} fusion(bf16[32,1,3072]{2,1,0:T(2,128)(2,1)} %reshape.96), kind=kLoop, calls=%fused_computation.21 | loop fusion | flops 193536 | bytes 208896 | tf_op jit(solution)/shard_map/reduce_sum | solution.py:70
  96.2 1.3 %add_convert_fusion = bf16[1,3072]{1,0:T(2,128)(2,1)} fusion(f32[1,3072]{1,0:T(1,128)S(1)} %bitcast.66, f32[1,3072]{1,0:T(1,128)S(1)} %bitcast.60, bf16[1,3072]{1,0:T(2,128)(2,1)} %param.15), kind=kLoop, calls=%fused_computation.38 | loop fusion | flops 18432 | bytes 36864 | tf_op jit(solution)/shard_map/convert_element_type | solution.py:71
Async XLA Ops:
  0.0 71.7 %copy-start = (bf16[1,576,3072]{2,1,0:T(8,128)(2,1)S(1)}, bf16[1,576,3072]{2,1,0:T(8,128)(2,1)}, u32[]{:S(2)}) copy-start(bf16[1,576,3072]{2,1,0:T(8,128)(2,1)} %param.27) | copy-start | bytes 10616836
  53.4 12.2 %all-to-all-start.2 = ((bf16[32,2,1536]{2,1,0:T(2,128)(2,1)}), bf16[32,2,1536]{2,1,0:T(2,128)(2,1)}, u32[]{:S(2)}, u32[]{:S(2)}) async-start(bf16[32,2,1536]{2,1,0:T(2,128)(2,1)} %reshape.93), calls=%async_computation.2 | async-start | bytes 393216 | tf_op jit(solution)/shard_map/all_to_all | solution.py:16

commit v2 on v1

v2 whole, which is shorter than its diff:
```python
import functools

import jax
import jax.numpy as jnp
from jax import lax
from jax.experimental import pallas as pl
from jax.experimental.pallas import tpu as pltpu
from jax.sharding import PartitionSpec as P

SPLIT = 8
LANES = 128
HEAD_BLOCKS = 4
WEIGHT_BLOCKS = 4
VMEM = pl.BlockSpec(memory_space=pltpu.VMEM)
HBM = pl.BlockSpec(memory_space=pltpu.HBM)
MIB = 1024 * 1024


def off_chip(*values):
    return [pltpu.with_memory_space_constraint(value, pltpu.HBM) for value in values]


def on_chip(*values):
    return [pltpu.with_memory_space_constraint(value, pltpu.VMEM) for value in values]


def call(body, out_shape, in_specs, scratch, flops, moved, limit):
    return pl.pallas_call(
        body,
        out_shape=out_shape,
        in_specs=in_specs,
        out_specs=jax.tree.map(lambda _: VMEM, out_shape),
        scratch_shapes=scratch,
        compiler_params=pltpu.CompilerParams(vmem_limit_bytes=limit),
        cost_estimate=pl.CostEstimate(flops=flops, bytes_accessed=moved, transcendentals=0),
    )


def exchange(blocks):
    return lax.all_to_all(blocks, "wide", split_axis=0, concat_axis=0, tiled=True)


def unfold(row_ref, held):
    for at in range(held.shape[0]):
        held[at : at + 1, :] = row_ref[0:1, at * LANES : (at + 1) * LANES].astype(jnp.float32)


def attention(
    query_ref, key_ref, value_ref, gate_ref, norm_ref, decay_ref, state_ref, resid_ref,
    moe_ref, ids_ref, weights_ref, w_out_ref, w_gate_ref,
    out_ref, resid_out, moe_out, coef_ref, w_out_copy, w_gate_copy,
    rows, norm_held, decay_held, states, resid_held, ids_held, weights_held,
    q_held, k_held, v_held, g_held, att, sems,
):
    heads = decay_held.shape[0]
    block = heads // HEAD_BLOCKS
    started = []

    def fetch(source, target):
        copy = pltpu.make_async_copy(source, target, sems.at[len(started)])
        copy.start()
        started.append(copy)
        return copy

    small = [fetch(ref, rows.at[at]) for at, ref in enumerate((query_ref, key_ref))]
    small.append(fetch(decay_ref, decay_held))
    parts = [pl.ds(at * block, block) for at in range(HEAD_BLOCKS)]
    read = [fetch(state_ref.at[0, part], states.at[part]) for part in parts]
    later = [fetch(ref, rows.at[2 + at]) for at, ref in enumerate((value_ref, gate_ref))]
    later.append(fetch(norm_ref, norm_held))
    later.append(fetch(resid_ref, resid_held))
    later.append(fetch(ids_ref, ids_held))
    later.append(fetch(weights_ref, weights_held))
    last = [fetch(moe_ref, moe_out), fetch(w_out_ref, w_out_copy), fetch(w_gate_ref, w_gate_copy)]

    for copy in small:
        copy.wait()
    unfold(rows.at[0], q_held)
    unfold(rows.at[1], k_held)
    q_rows = q_held[...]
    q_columns = q_rows.T
    both = jnp.sum(q_rows * k_held[...], axis=1, keepdims=True)
    for at in range(HEAD_BLOCKS):
        read[at].wait()
        for head in range(at * block, (at + 1) * block):
            seen = jnp.sum(q_columns[:, head : head + 1] * states[head], axis=0, keepdims=True)
            fade = jnp.exp(jnp.full((1, LANES), -decay_held[head], jnp.float32))
            att[head : head + 1, :] = fade * seen
    for copy in later:
        copy.wait()
    unfold(rows.at[2], v_held)
    unfold(rows.at[3], g_held)
    found = att[...] + both * v_held[...]
    scale = lax.rsqrt(jnp.sum(found * found, keepdims=True) / found.size + 1e-06)
    out_ref[...] = found * scale * norm_held[...] * jax.nn.sigmoid(g_held[...])

    unfold(resid_held, resid_out)
    owner = lax.axis_index("wide") // SPLIT
    named = jnp.where(ids_held[...] == owner, weights_held[...], 0.0)
    along = jnp.sum(named, axis=0, keepdims=True)
    square = (coef_ref.shape[0], coef_ref.shape[0])
    same = lax.broadcasted_iota(jnp.int32, square, 0) == lax.broadcasted_iota(jnp.int32, square, 1)
    column = jnp.sum(jnp.where(same, along, 0.0), axis=1, keepdims=True)
    coef_ref[...] = jnp.broadcast_to(column, coef_ref.shape)
    for copy in last:
        copy.wait()


def rows_to_blocks(spread, out_ref):
    rows, tiles, _ = out_ref.shape
    for row in range(rows):
        out_ref[row] = spread[pl.ds(row * tiles, tiles), :].astype(out_ref.dtype)


def project(columns_ref, w_ref, out_ref, spread):
    rows, tiles, _ = out_ref.shape
    made = jnp.dot(
        columns_ref[...].astype(jnp.bfloat16), w_ref[...], preferred_element_type=jnp.float32
    )
    for tile in range(tiles):
        spread[pl.ds(tile, rows, stride=tiles), :] = made[:, tile * LANES : (tile + 1) * LANES]
    rows_to_blocks(spread, out_ref)


def add_up(parts_ref):
    total = parts_ref[0].astype(jnp.float32)
    for at in range(1, parts_ref.shape[0]):
        total = total + parts_ref[at].astype(jnp.float32)
    return total


def middle(parts_ref, resid_ref, gain_ref, hid_ref, copies_ref):
    hid = (resid_ref[...] + add_up(parts_ref)).astype(jnp.bfloat16).astype(jnp.float32)
    hid_ref[...] = hid
    scale = lax.rsqrt(jnp.sum(hid * hid, keepdims=True) / hid.size + 1e-06)
    normed = (hid * scale * gain_ref[...]).astype(jnp.bfloat16)
    for at in range(copies_ref.shape[0]):
        copies_ref[at] = normed


def experts(
    blocks_ref, coef_ref, gate_ref, up_ref, down_ref, out_ref, spread, inputs, up, down, sems
):
    rows, tiles, _ = out_ref.shape
    hidden = gate_ref.shape[0]
    block = hidden // WEIGHT_BLOCKS
    parts = [pl.ds(at * block, block) for at in range(WEIGHT_BLOCKS)]
    copies = []
    for source, target in ((up_ref, up), (down_ref, down)):
        for part in parts:
            copy = pltpu.make_async_copy(source.at[0, part], target.at[part], sems.at[len(copies)])
            copy.start()
            copies.append(copy)
    for row in range(rows):
        spread[pl.ds(row * tiles, tiles), :] = blocks_ref[row].astype(jnp.float32)
    for tile in range(tiles):
        inputs[:, tile * LANES : (tile + 1) * LANES] = spread[
            pl.ds(tile, rows, stride=tiles), :
        ].astype(jnp.bfloat16)
    given = inputs[...]
    by_rows = functools.partial(
        lax.dot_general,
        dimension_numbers=(((1,), (1,)), ((), ())),
        preferred_element_type=jnp.float32,
    )
    gate = jax.nn.silu(by_rows(given, gate_ref[...]))
    for copy in copies[:WEIGHT_BLOCKS]:
        copy.wait()
    inner = (gate * by_rows(given, up[...])).astype(jnp.bfloat16)
    for copy in copies[WEIGHT_BLOCKS:]:
        copy.wait()
    made = jnp.dot(inner, down[...], preferred_element_type=jnp.float32)
    coef = coef_ref[...]
    for tile in range(tiles):
        spread[pl.ds(tile, rows, stride=tiles), :] = (
            made[:, tile * LANES : (tile + 1) * LANES] * coef
        )
    rows_to_blocks(spread, out_ref)


def finish(parts_ref, hid_ref, out_ref):
    mixed = hid_ref[...] + add_up(parts_ref)
    for at in range(mixed.shape[0]):
        out_ref[0:1, at * LANES : (at + 1) * LANES] = mixed[at : at + 1, :].astype(out_ref.dtype)


def shards(
    resid,
    query,
    key,
    value,
    state,
    decay,
    out_gate,
    norm_gain,
    w_out,
    moe_gain,
    w_gate,
    w_up,
    w_down,
    expert_ids,
    expert_weights,
):
    width = resid.shape[1]
    heads = decay.shape[0]
    features = query.shape[1]
    devices = lax.axis_size("wide")
    tiles = width // LANES
    hidden = w_gate.shape[1]
    f32, bf16 = jnp.float32, jnp.bfloat16
    row = pltpu.VMEM((tiles, LANES), f32)
    blocks = pltpu.VMEM((devices, tiles, LANES), bf16)
    spread = pltpu.VMEM((devices * tiles, LANES), f32)
    per_head = pltpu.VMEM((heads, LANES), f32)

    attn, resid_rows, moe_rows, coef, w_out_held, w_gate_held = call(
        attention,
        (
            per_head,
            row,
            row,
            pltpu.VMEM((devices, LANES), f32),
            pltpu.VMEM(w_out.shape, bf16),
            pltpu.VMEM(w_gate.shape[1:], bf16),
        ),
        [HBM] * 13,
        [
            pltpu.VMEM((4, 1, features), bf16),
            per_head,
            pltpu.SMEM((heads,), f32),
            pltpu.VMEM(state.shape[1:], f32),
            pltpu.VMEM((1, width), bf16),
            pltpu.VMEM((2, devices), jnp.int32),
            pltpu.VMEM((2, devices), f32),
        ]
        + [per_head] * 5
        + [pltpu.SemaphoreType.DMA((12 + HEAD_BLOCKS,))],
        2 * state.size,
        4 * state.size,
        8 * MIB,
    )(
        *off_chip(
            query,
            key,
            value,
            out_gate,
            norm_gain.reshape(heads, LANES),
            decay,
            state,
            resid,
            moe_gain.reshape(tiles, LANES),
            expert_ids.T,
            expert_weights.T,
            w_out,
            w_gate.reshape(w_gate.shape[1:]),
        )
    )
    columns = exchange(attn.reshape(devices, 1, features // devices))
    parts = call(
        project, blocks, [VMEM] * 2, [spread], 2 * devices * w_out.size, 2 * w_out.size, 4 * MIB
    )(*on_chip(columns.reshape(devices, features // devices), w_out_held))
    hid, copies = call(
        middle, (row, blocks), [VMEM] * 3, [], devices * width, 4 * devices * width, 2 * MIB
    )(*on_chip(exchange(parts), resid_rows, moe_rows))
    weight = pltpu.VMEM((hidden, width), bf16)
    outcome = call(
        experts,
        blocks,
        [VMEM] * 3 + [HBM] * 2,
        [
            spread,
            pltpu.VMEM((devices, width), bf16),
            weight,
            weight,
            pltpu.SemaphoreType.DMA((2 * WEIGHT_BLOCKS,)),
        ],
        6 * devices * hidden * width,
        6 * hidden * width,
        16 * MIB,
    )(*on_chip(exchange(copies), coef, w_gate_held), *off_chip(w_up, w_down))
    return call(
        finish,
        jax.ShapeDtypeStruct((1, width), bf16),
        [VMEM, VMEM],
        [],
        devices * width,
        2 * devices * width,
        2 * MIB,
    )(*on_chip(exchange(outcome), hid))


def solution(mesh):
    return jax.shard_map(
        shards,
        mesh=mesh,
        in_specs=(
            P(("group", "wide"), None),
            P(("group", "wide"), None),
            P(("group", "wide"), None),
            P(("group", "wide"), None),
            P(("group", "wide"), None, None, None),
            P(),
            P(("group", "wide"), None),
            P(),
            P("wide", None),
            P(),
            P("wide", None, None),
            P("wide", None, None),
            P("wide", None, None),
            P("group", None),
            P("group", None),
        ),
        out_specs=P(("group", "wide"), None),
        check_vma=False,
    )
```

time: 98.7 us -> 56.3 us (0.57)
  other arithmetic: 19.5 us -> 0 us
  local copies, waits for them, and re-layouts: 13.4 us -> 0 us
  matrix products: 12.9 us -> 0 us
  blocking collectives: 38.7 us -> 47.6 us
  Pallas kernels: 0 us -> 8.39 us
  waiting for transfers between devices: 8.21 us -> 0 us
  starting transfers between devices: 3.28 us -> 0 us
  between operations: 1.48 us -> 0.03 us
    all_to_all x2 -> x4, blocking collectives: 24.4 us -> 47.6 us  [exchange(): lax.all_to_all(blocks, 'wide', split_axis=0, concat_axis=0, tiled=True)]
    all_to_all x1 -> x0, blocking collectives: 14.3 us -> none  [shards(): lax.all_to_all(attn, 'wide', split_axis=1, concat_axis=0, tiled=True)]
    dot_general x4 -> x0, matrix products: 12.9 us -> none  [the longest x1 4.59 us: shards(): jnp.dot(inner, w_down[0], preferred_element_type=jnp.float32)]
    unnamed x8 -> x0, local copies, waits for them, and re-layouts: 11.9 us -> none
    pallas_call x0 -> x5, Pallas kernels: none -> 8.39 us  [the longest x1 4.19 us: shards(): call(experts, blocks, [VMEM] * 3 + [HBM] * 2, [spread, pltpu.VMEM((device...]
    all_to_all x1 -> x0, waiting for transfers between devices: 8.21 us -> none  [exchange(): lax.all_to_all(blocks, 'wide', split_axis=0, concat_axis=0, tiled=True)]
    reduce_sum x5 -> x0, other arithmetic: 5.45 us -> none  [the longest x1 1.42 us: shards(): jnp.mean(hid_f * hid_f, axis=1, keepdims=True) + 1e-06]
    reshape x2 -> x0, other arithmetic: 4.65 us -> none  [the longest x1 2.32 us: shards(): parts = exchange(proj.reshape(devices, local_rows, width))]
  transfers between devices with their start and end apart: 1 -> 0, of which waited for: 1 -> 0; matrix products, arithmetic and copies ran while one was open for 1% -> 0% of each run, Pallas kernels for 0% -> 0%
where the time goes in v2:
time: 56.3 us; the launch traced here: 56 us
  blocking collectives  47.6 us (85%)
  Pallas kernels  8.39 us (15%)
    all_to_all x4, blocking collectives, exchange(): lax.all_to_all(blocks, 'wide', split_axis=0, concat_axis=0, tiled=True)  47.6 us
    pallas_call x1, Pallas kernels, shards(): call(experts, blocks, [VMEM] * 3 + [HBM] * 2, [spread, pltpu.VMEM((device...  4.19 us
    pallas_call x1, Pallas kernels, shards(): call(attention, (per_head, row, row, pltpu.VMEM((devices, LANES), f32), p...  3.11 us

profile of v2, /device:TPU:0, one launch (start us, length us, event | category | flops | bytes accessed | tf_op | source)
XLA Modules:
  0.0 56.0 jit_solution(1766171592124026786)
XLA Ops:
  0.0 3.1 %shard_map.145 = (f32[32,128]{1,0:T(8,128)S(1)}, f32[24,128]{1,0:T(8,128)S(1)}, f32[24,128]{1,0:T(8,128)S(1)}, f32[32,128]{1,0:T(8,128)S(1)}, bf16[128,3072]{1,0...) custom-call(bf16[1,4096]{1,0:T(2,128)(2,1)} %query_ref.1, bf16[1,4096]{1,0:T(2,128)(2,1)} %key_ref.1, ...), custom_call_target="tpu_custom_call" | custom-call | flops 1048576 | bytes 2097152 | tf_op jit(solution)/shard_map/pallas_call | solution.py:216
  3.1 14.3 %all_to_all.20 = f32[32,1,128]{2,1,0:T(1,128)S(1)} all-to-all(f32[32,1,128]{2,1,0:T(1,128)S(1)} %bitcast.10), channel_id=1, replica_groups=mesh['group'=1,'wide'=32] {'wide'}, dimensions={0} | all-to-all | bytes 32768 | tf_op jit(solution)/shard_map/all_to_all | solution.py:40
  17.4 0.3 shard_map.146
  17.7 10.7 %all_to_all.21.parts_ref = bf16[32,24,128]{2,1,0:T(8,128)(2,1)S(1)} all-to-all(bf16[32,24,128]{2,1,0:T(8,128)(2,1)S(1)} %shard_map.146), channel_id=1, replica_groups=mesh['group'=1,'wide'=32] {'wide'}, dimensions={0} | all-to-all | bytes 393216 | tf_op jit(solution)/shard_map/all_to_all | solution.py:40
  28.4 0.2 shard_map.147
  28.5 11.3 %all_to_all.22.blocks_ref = bf16[32,24,128]{2,1,0:T(8,128)(2,1)S(1)} all-to-all(bf16[32,24,128]{2,1,0:T(8,128)(2,1)S(1)} %get-tuple-element.17), channel_id=1, replica_groups=mesh['group'=1,'wide'=32] {'wide'}, dimensions={0} | all-to-all | bytes 393216 | tf_op jit(solution)/shard_map/all_to_all | solution.py:40
  39.8 4.2 %shard_map.148 = bf16[32,24,128]{2,1,0:T(8,128)(2,1)S(1)} custom-call(bf16[32,24,128]{2,1,0:T(8,128)(2,1)S(1)} %all_to_all.22.blocks_ref, f32[32,128]{1,0:T(8,128)S(1)} %get-tuple-element.18.coef_ref, bf16[576,3072]{1,0:T(8,128)(2,1)S(1)} %get-tuple-element.19.gate_ref, bf16[1,576,3072]{2,1,0:T(8,128)(2,1)} %up_ref.1, bf16[1,576,3072]{2,1,0:T(8,128)(2,1)} %down_ref.1), custom_call_target="tpu_custom_call" | custom-call | flops 339738624 | bytes 10616832 | tf_op jit(solution)/shard_map/pallas_call | solution.py:266
  44.0 11.4 %all_to_all.23.parts_ref = bf16[32,24,128]{2,1,0:T(8,128)(2,1)S(1)} all-to-all(bf16[32,24,128]{2,1,0:T(8,128)(2,1)S(1)} %shard_map.148), channel_id=1, replica_groups=mesh['group'=1,'wide'=32] {'wide'}, dimensions={0} | all-to-all | bytes 393216 | tf_op jit(solution)/shard_map/all_to_all | solution.py:40
  55.4 0.7 %shard_map.149 = bf16[1,3072]{1,0:T(2,128)(2,1)} custom-call(bf16[32,24,128]{2,1,0:T(8,128)(2,1)S(1)} %all_to_all.23.parts_ref, f32[24,128]{1,0:T(8,128)S(1)} %get-tuple-element.20.hid_ref), custom_call_target="tpu_custom_call" | custom-call | flops 98304 | bytes 196608 | tf_op jit(solution)/shard_map/pallas_call | solution.py:281

commit v3 on v2

v3 whole, which is shorter than its diff:
```python
import jax
import jax.numpy as jnp
from jax import lax
from jax.experimental import pallas as pl
from jax.experimental.pallas import tpu as pltpu
from jax.sharding import PartitionSpec as P

SPLIT = 8
LANES = 128
HEAD_BLOCKS = 4
VMEM = pl.BlockSpec(memory_space=pltpu.VMEM)
HBM = pl.BlockSpec(memory_space=pltpu.HBM)
MIB = 1024 * 1024


def off_chip(*values):
    return [pltpu.with_memory_space_constraint(value, pltpu.HBM) for value in values]


def on_chip(*values):
    return [pltpu.with_memory_space_constraint(value, pltpu.VMEM) for value in values]


def call(body, out_shape, in_specs, scratch, flops, moved, limit):
    return pl.pallas_call(
        body,
        out_shape=out_shape,
        in_specs=in_specs,
        out_specs=jax.tree.map(lambda _: VMEM, out_shape),
        scratch_shapes=scratch,
        compiler_params=pltpu.CompilerParams(vmem_limit_bytes=limit),
        cost_estimate=pl.CostEstimate(flops=flops, bytes_accessed=moved, transcendentals=0),
    )


def exchange(blocks):
    return lax.all_to_all(blocks, "wide", split_axis=0, concat_axis=0, tiled=True)


def own_half(ref):
    half = ref.shape[1] // 2
    return pl.ds(pl.multiple_of(lax.rem(lax.axis_index("wide"), 2) * half, half), half)


def other_half(ref):
    half = ref.shape[1] // 2
    return pl.ds(pl.multiple_of((1 - lax.rem(lax.axis_index("wide"), 2)) * half, half), half)


def swap(value):
    devices = lax.axis_size("wide")
    return lax.ppermute(value, "wide", [(at, at ^ 1) for at in range(devices)])


def unfold(row_ref, held):
    for at in range(held.shape[0]):
        held[at : at + 1, :] = row_ref[0:1, at * LANES : (at + 1) * LANES].astype(jnp.float32)


def attention(
    query_ref, key_ref, value_ref, gate_ref, norm_ref, decay_ref, state_ref, resid_ref,
    moe_ref, ids_ref, weights_ref, w_out_ref,
    out_ref, resid_out, moe_out, coef_ref, w_out_half,
    rows, norm_held, decay_held, states, resid_held, ids_held, weights_held,
    q_held, k_held, v_held, g_held, att, sems,
):
    heads = decay_held.shape[0]
    block = heads // HEAD_BLOCKS
    started = []

    def fetch(source, target):
        copy = pltpu.make_async_copy(source, target, sems.at[len(started)])
        copy.start()
        started.append(copy)
        return copy

    small = [fetch(ref, rows.at[at]) for at, ref in enumerate((query_ref, key_ref))]
    small.append(fetch(decay_ref, decay_held))
    parts = [pl.ds(at * block, block) for at in range(HEAD_BLOCKS)]
    read = [fetch(state_ref.at[0, part], states.at[part]) for part in parts]
    later = [fetch(ref, rows.at[2 + at]) for at, ref in enumerate((value_ref, gate_ref))]
    later.append(fetch(norm_ref, norm_held))
    later.append(fetch(resid_ref, resid_held))
    later.append(fetch(ids_ref, ids_held))
    later.append(fetch(weights_ref, weights_held))
    last = [fetch(moe_ref, moe_out), fetch(w_out_ref.at[:, own_half(w_out_ref)], w_out_half)]

    for copy in small:
        copy.wait()
    unfold(rows.at[0], q_held)
    unfold(rows.at[1], k_held)
    q_rows = q_held[...]
    q_columns = q_rows.T
    both = jnp.sum(q_rows * k_held[...], axis=1, keepdims=True)
    for at in range(HEAD_BLOCKS):
        read[at].wait()
        for head in range(at * block, (at + 1) * block):
            seen = jnp.sum(q_columns[:, head : head + 1] * states[head], axis=0, keepdims=True)
            fade = jnp.exp(jnp.full((1, LANES), -decay_held[head], jnp.float32))
            att[head : head + 1, :] = fade * seen
    for copy in later:
        copy.wait()
    unfold(rows.at[2], v_held)
    unfold(rows.at[3], g_held)
    found = att[...] + both * v_held[...]
    scale = lax.rsqrt(jnp.sum(found * found, keepdims=True) / found.size + 1e-06)
    made = found * scale * norm_held[...] * jax.nn.sigmoid(g_held[...])
    if out_ref.shape[0] == heads:
        out_ref[...] = made
    else:
        att[...] = made
        for core in range(2):
            of_core = att[pl.ds(core, heads // 2, stride=2), :]
            out_ref[pl.ds(core, heads // 2, stride=4), :] = of_core
            out_ref[pl.ds(core + 2, heads // 2, stride=4), :] = of_core

    unfold(resid_held, resid_out)
    owner = lax.axis_index("wide") // SPLIT
    named = jnp.where(ids_held[...] == owner, weights_held[...], 0.0)
    along = jnp.sum(named, axis=0, keepdims=True)
    square = (coef_ref.shape[0], coef_ref.shape[0])
    same = lax.broadcasted_iota(jnp.int32, square, 0) == lax.broadcasted_iota(jnp.int32, square, 1)
    column = jnp.sum(jnp.where(same, along, 0.0), axis=1, keepdims=True)
    coef_ref[...] = jnp.broadcast_to(column, coef_ref.shape)
    for copy in last:
        copy.wait()


def columns_to_blocks(made, spread, out_ref):
    rows, groups, size, _ = out_ref.shape
    tiles = groups * size
    for tile in range(tiles):
        spread[pl.ds(tile, rows, stride=tiles), :] = made[:, tile * LANES : (tile + 1) * LANES]
    for row in range(rows):
        for group in range(groups):
            lines = spread[pl.ds(row * tiles + group * size, size), :]
            out_ref[row, group] = lines.astype(out_ref.dtype)


def blocks_to_columns(blocks_ref, spread, inputs):
    rows, groups, size, _ = blocks_ref.shape
    tiles = groups * size
    for row in range(rows):
        for group in range(groups):
            lines = pl.ds(row * tiles + group * size, size)
            spread[lines, :] = blocks_ref[row, group].astype(jnp.float32)
    for tile in range(tiles):
        inputs[:, tile * LANES : (tile + 1) * LANES] = spread[
            pl.ds(tile, rows, stride=tiles), :
        ].astype(jnp.bfloat16)
    return inputs[...]


def multiply(left, right):
    return jnp.dot(left, right, preferred_element_type=jnp.float32)


def by_rows(left, weight):
    return lax.dot_general(
        left, weight, (((1,), (1,)), ((), ())), preferred_element_type=jnp.float32
    )


def project(*refs):
    *column_refs, w_ref, w_other_ref, out_ref, spread = refs
    rows = out_ref.shape[0]
    if len(column_refs) == 1:
        pair = [column_refs[0][pl.ds(core, rows, stride=2), :] for core in range(2)]
    else:
        pair = [ref[...] for ref in column_refs]
    first = lax.rem(lax.axis_index("wide"), 2) == 0
    own = jnp.where(first, pair[0], pair[1]).astype(jnp.bfloat16)
    other = jnp.where(first, pair[1], pair[0]).astype(jnp.bfloat16)
    made = multiply(own, w_ref[...]) + multiply(other, w_other_ref[:, own_half(w_other_ref)])
    columns_to_blocks(made, spread, out_ref)


def add_up(parts_ref, held):
    devices, groups, size, _ = parts_ref.shape
    for half in range(2):
        total = parts_ref[half].astype(jnp.float32)
        for at in range(half + 2, devices, 2):
            total = total + parts_ref[at].astype(jnp.float32)
        for group in range(groups):
            start = (half * groups + group) * size
            held[start : start + size, :] = total[group]


def middle(parts_ref, resid_ref, gain_ref, hid_ref, copies_ref, held):
    devices, groups, size, _ = copies_ref.shape
    add_up(parts_ref, held)
    hid = (resid_ref[...] + held[...]).astype(jnp.bfloat16).astype(jnp.float32)
    hid_ref[...] = hid
    scale = lax.rsqrt(jnp.sum(hid * hid, keepdims=True) / hid.size + 1e-06)
    held[...] = hid * scale * gain_ref[...]
    for half in range(2):
        for group in range(groups):
            start = (half * groups + group) * size
            lines = held[start : start + size, :].astype(jnp.bfloat16)
            for at in range(half, devices, 2):
                copies_ref[at, group] = lines


def experts_own(blocks_ref, gate_ref, up_ref, gate_out, up_out, up_own, up_other, spread, inputs, sems):
    half = up_own.shape[1]
    copies = []
    for columns, target in ((own_half(gate_ref), up_own), (other_half(gate_ref), up_other)):
        copy = pltpu.make_async_copy(up_ref.at[0, :, columns], target, sems.at[len(copies)])
        copy.start()
        copies.append(copy)
    given = blocks_to_columns(blocks_ref, spread, inputs)
    gate_out[...] = by_rows(given, gate_ref[:, own_half(gate_ref)])
    copies[0].wait()
    up_out[...] = by_rows(given, up_own[...])
    copies[1].wait()


def experts_other(
    blocks_ref, gate_ref, up_other, gate_held, up_held, coef_ref, down_ref,
    inner_ref, send_ref, down_own, down_other, spread, inputs, sems,
):
    copies = []
    for columns, target in ((other_half(gate_ref), down_other), (own_half(gate_ref), down_own)):
        copy = pltpu.make_async_copy(down_ref.at[0, :, columns], target, sems.at[len(copies)])
        copy.start()
        copies.append(copy)
    given = blocks_to_columns(blocks_ref, spread, inputs)
    gate = gate_held[...] + by_rows(given, gate_ref[:, other_half(gate_ref)])
    upper = up_held[...] + by_rows(given, up_other[...])
    inner = (jax.nn.silu(gate) * upper).astype(jnp.bfloat16)
    inner_ref[...] = inner
    copies[0].wait()
    made = multiply(inner, down_other[...])
    coef = coef_ref[...]
    for at in range(0, made.shape[1], LANES):
        send_ref[:, at : at + LANES] = (made[:, at : at + LANES] * coef).astype(send_ref.dtype)
    copies[1].wait()


def experts_last(inner_ref, coef_ref, down_own, out_ref):
    made = multiply(inner_ref[...], down_own[...])
    coef = coef_ref[...]
    for at in range(0, made.shape[1], LANES):
        out_ref[:, at : at + LANES] = made[:, at : at + LANES] * coef


def join(own_ref, other_ref, out_ref, spread):
    columns_to_blocks(own_ref[...] + other_ref[...].astype(jnp.float32), spread, out_ref)


def finish(parts_ref, hid_ref, out_ref, held):
    add_up(parts_ref, held)
    held[...] = hid_ref[...] + held[...]
    for at in range(held.shape[0]):
        out_ref[0:1, at * LANES : (at + 1) * LANES] = held[at : at + 1, :].astype(out_ref.dtype)


def shards(
    resid,
    query,
    key,
    value,
    state,
    decay,
    out_gate,
    norm_gain,
    w_out,
    moe_gain,
    w_gate,
    w_up,
    w_down,
    expert_ids,
    expert_weights,
):
    width = resid.shape[1]
    half = width // 2
    heads = decay.shape[0]
    features = query.shape[1]
    devices = lax.axis_size("wide")
    each = features // devices
    tiles = width // LANES
    hidden = w_gate.shape[1]
    size = next(size for size in (8, 4, 2, 1) if tiles // 2 % size == 0)
    f32, bf16 = jnp.float32, jnp.bfloat16
    row = pltpu.VMEM((tiles, LANES), f32)
    blocks = pltpu.VMEM((devices, tiles // 2 // size, size, LANES), bf16)
    spread = pltpu.VMEM((devices * tiles // 2, LANES), f32)
    per_head = pltpu.VMEM((heads, LANES), f32)
    paired = each == LANES

    attn, resid_rows, moe_rows, coef, w_out_half = call(
        attention,
        (
            pltpu.VMEM((2 * heads if paired else heads, LANES), f32),
            row,
            row,
            pltpu.VMEM((devices, LANES), f32),
            pltpu.VMEM((each, half), bf16),
        ),
        [HBM] * 12,
        [
            pltpu.VMEM((4, 1, features), bf16),
            per_head,
            pltpu.SMEM((heads,), f32),
            pltpu.VMEM(state.shape[1:], f32),
            pltpu.VMEM((1, width), bf16),
            pltpu.VMEM((2, devices), jnp.int32),
            pltpu.VMEM((2, devices), f32),
        ]
        + [per_head] * 5
        + [pltpu.SemaphoreType.DMA((11 + HEAD_BLOCKS,))],
        2 * state.size,
        4 * state.size,
        8 * MIB,
    )(
        *off_chip(
            query,
            key,
            value,
            out_gate,
            norm_gain.reshape(heads, LANES),
            decay,
            state,
            resid,
            moe_gain.reshape(tiles, LANES),
            expert_ids.T,
            expert_weights.T,
            w_out,
        )
    )
    w_out_other = swap(w_out)
    if paired:
        columns = exchange(attn.reshape(devices, 2, LANES))
        columns = [columns.reshape(2 * devices, LANES)]
    else:
        attn = jnp.repeat(attn.reshape(devices // 2, 2, each), 2, axis=0)
        columns = exchange(attn)
        columns = [columns[:, core] for core in range(2)]
    parts = call(
        project,
        blocks,
        [VMEM] * (2 + len(columns)),
        [spread],
        2 * devices * w_out.size,
        2 * w_out.size,
        4 * MIB,
    )(*on_chip(*columns, w_out_half, w_out_other))
    hid, copies = call(
        middle, (row, blocks), [VMEM] * 3, [row], devices * width, 4 * devices * width, 2 * MIB
    )(*on_chip(exchange(parts), resid_rows, moe_rows))
    given = exchange(copies)
    given_other = swap(given)
    inputs = pltpu.VMEM((devices, half), bf16)
    partial_sum = pltpu.VMEM((devices, hidden), f32)
    weight = pltpu.VMEM((hidden, half), bf16)
    gate_weight = w_gate.reshape(w_gate.shape[1:])
    *sums, up_other = call(
        lambda blocks_ref, gate_ref, up_ref, gate_out, up_out, up_other, *rest: experts_own(
            blocks_ref, gate_ref, up_ref, gate_out, up_out, rest[0], up_other, *rest[1:]
        ),
        (partial_sum, partial_sum, weight),
        [VMEM] * 2 + [HBM],
        [weight, spread, inputs, pltpu.SemaphoreType.DMA((2,))],
        2 * devices * hidden * width,
        4 * hidden * width,
        8 * MIB,
    )(*on_chip(given, gate_weight), *off_chip(w_up))
    inner, send, down_own = call(
        experts_other,
        (pltpu.VMEM((devices, hidden), bf16), inputs, weight),
        [VMEM] * 6 + [HBM],
        [weight, spread, inputs, pltpu.SemaphoreType.DMA((2,))],
        3 * devices * hidden * width,
        4 * hidden * width,
        8 * MIB,
    )(*on_chip(given_other, gate_weight, up_other, *sums, coef), *off_chip(w_down))
    received = swap(send)
    own = call(
        experts_last,
        pltpu.VMEM((devices, half), f32),
        [VMEM] * 3,
        [],
        devices * hidden * width,
        hidden * width,
        4 * MIB,
    )(*on_chip(inner, coef, down_own))
    outcome = call(
        join, blocks, [VMEM] * 2, [spread], devices * width, 4 * devices * width, 4 * MIB
    )(*on_chip(own, received))
    return call(
        finish,
        jax.ShapeDtypeStruct((1, width), bf16),
        [VMEM, VMEM],
        [row],
        devices * width,
        2 * devices * width,
        2 * MIB,
    )(*on_chip(exchange(outcome), hid))


def solution(mesh):
    return jax.shard_map(
        shards,
        mesh=mesh,
        in_specs=(
            P(("group", "wide"), None),
            P(("group", "wide"), None),
            P(("group", "wide"), None),
            P(("group", "wide"), None),
            P(("group", "wide"), None, None, None),
            P(),
            P(("group", "wide"), None),
            P(),
            P("wide", None),
            P(),
            P("wide", None, None),
            P("wide", None, None),
            P("wide", None, None),
            P("group", None),
            P("group", None),
        ),
        out_specs=P(("group", "wide"), None),
        check_vma=False,
    )
```

time: 56.3 us -> 52.9 us (0.940)
  blocking collectives: 47.6 us -> 42.5 us
  starting transfers between devices: 0 us -> 1.07 us
    all_to_all x4, blocking collectives: 47.6 us -> 42.5 us  [exchange(): lax.all_to_all(blocks, 'wide', split_axis=0, concat_axis=0, tiled=True)]
    ppermute x0 -> x3, starting transfers between devices: none -> 1.07 us  [swap(): return lax.ppermute(value, 'wide', [(at, at ^ 1) for at in range(devices)])]
    pallas_call x5 -> x8, Pallas kernels: 8.39 us -> 8.5 us  [the longest x1 2.52 us: shards(): call(attention, (pltpu.VMEM((2 * heads if paired else heads, LANES), f32)...]
  transfers between devices with their start and end apart: 0 -> 3, of which waited for: 0 -> 1; matrix products, arithmetic and copies ran while one was open for 0% -> 0% of each run, Pallas kernels for 0% -> 10%
where the time goes in v3:
time: 52.9 us; the launch traced here: 52.7 us
  blocking collectives  42.5 us (80%)
  Pallas kernels  8.5 us (16%)
  starting transfers between devices  1.07 us (2%)
  waiting for transfers between devices  0.56 us (1%)
    all_to_all x4, blocking collectives, exchange(): lax.all_to_all(blocks, 'wide', split_axis=0, concat_axis=0, tiled=True)  42.5 us
    pallas_call x1, Pallas kernels, shards(): call(attention, (pltpu.VMEM((2 * heads if paired else heads, LANES), f32)...  2.52 us
    pallas_call x1, Pallas kernels, shards(): call(experts_other, (pltpu.VMEM((devices, hidden), bf16), inputs, weight)...  2.25 us
    pallas_call x1, Pallas kernels, shards(): call(lambda blocks_ref, gate_ref, up_ref, gate_out, up_out, up_other, *re...  2.19 us
    ppermute x3, starting transfers between devices, swap(): return lax.ppermute(value, 'wide', [(at, at ^ 1) for at in range(devices)])  1.07 us
  transfers between devices with their start and end apart: 3, of which 1 were waited for; matrix products, arithmetic and copies ran while one was open for 0% of the time, Pallas kernels for 10%

profile of v3, /device:TPU:0, one launch (start us, length us, event | category | flops | bytes accessed | tf_op | source)
XLA Modules:
  0.0 52.7 jit_solution(17328417121428743921)
XLA Ops:
  0.0 0.0 copy-start
  0.0 0.5 collective-permute-start
  0.5 2.5 %shard_map.145 = (f32[64,128]{1,0:T(8,128)S(1)}, f32[24,128]{1,0:T(8,128)S(1)}, f32[24,128]{1,0:T(8,128)S(1)}, f32[32,128]{1,0:T(8,128)S(1)}, bf16[128,1536]{1,0:T(8,128)(2,1)S(1)}) custom-call(bf16[1,4096]{1,0:T(2,128)(2,1)} %query_ref.1, bf16[1,4096]{1,0:T(2,128)(2,1)} %key_ref.1, bf16[1,4096]{1,0:T(2,128)(2,1)} %value_ref.1, bf16[1,4096]{1,0:T(2,128)(2,1)} %gate_ref.1, ...), custom_call_target="tpu_custom_call" | custom-call | flops 1048576 | bytes 2097152 | tf_op jit(solution)/shard_map/pallas_call | solution.py:291
  3.0 14.1 %all_to_all.20 = f32[32,2,128]{2,1,0:T(2,128)S(1)} all-to-all(f32[32,2,128]{2,1,0:T(2,128)S(1)} %bitcast.10), channel_id=1, replica_groups=mesh['group'=1,'wide'=32] {'wide'}, dimensions={0} | all-to-all | bytes 65536 | tf_op jit(solution)/shard_map/all_to_all | solution.py:37
  17.1 0.0 collective-permute-done.refs_2_
  17.1 0.3 shard_map.146
  17.4 9.5 %all_to_all.21.parts_ref = bf16[32,3,4,128]{3,2,1,0:T(4,128)(2,1)S(1)} all-to-all(bf16[32,3,4,128]{3,2,1,0:T(4,128)(2,1)S(1)} %shard_map.146), channel_id=1, replica_groups=mesh['group'=1,'wide'=32] {'wide'}, dimensions={0} | all-to-all | bytes 196608 | tf_op jit(solution)/shard_map/all_to_all | solution.py:37
  26.9 0.2 shard_map.147
  27.1 9.5 %all_to_all.22.blocks_ref = bf16[32,3,4,128]{3,2,1,0:T(4,128)(2,1)S(1)} all-to-all(bf16[32,3,4,128]{3,2,1,0:T(4,128)(2,1)S(1)} %get-tuple-element.22), channel_id=1, replica_groups=mesh['group'=1,'wide'=32] {'wide'}, dimensions={0} | all-to-all | bytes 196608 | tf_op jit(solution)/shard_map/all_to_all | solution.py:37
  36.6 0.1 collective-permute-start.1
  36.7 0.0 copy-done
  36.7 2.2 %shard_map.148 = (f32[32,576]{1,0:T(8,128)S(1)}, f32[32,576]{1,0:T(8,128)S(1)}, bf16[576,1536]{1,0:T(8,128)(2,1)S(1)}) custom-call(bf16[32,3,4,128]{3,2,1,0:T(4,128)(2,1)S(1)} %all_to_all.22.blocks_ref, bf16[576,3072]{1,0:T(8,128)(2,1)S(1)} %bitcast.7, bf16[1,576,3072]{2,1,0:T(8,128)(2,1)} %up_ref.1), custom_call_target="tpu_custom_call" | custom-call | flops 113246208 | bytes 7077888 | tf_op jit(solution)/shard_map/pallas_call | solution.py:357
  38.9 0.0 collective-permute-done.1.blocks_ref
  38.9 2.3 %shard_map.149 = (bf16[32,576]{1,0:T(8,128)(2,1)S(1)}, bf16[32,1536]{1,0:T(8,128)(2,1)S(1)}, bf16[576,1536]{1,0:T(8,128)(2,1)S(1)}) custom-call(bf16[32,3,4,128]{3,2,1,0:T(4,128)(2,1)S(1)} %collective-permute-done.1.blocks_ref, bf16[576,3072]{1,0:T(8,128)(2,1)S(1)} %bitcast.8, bf16[576,1536]{1,0:T(8,128)(2,1)S(1)} %get-tuple-element.23.up_other, ...), custom_call_target="tpu_custom_call" | custom-call | flops 169869312 | bytes 7077888 | tf_op jit(solution)/shard_map/pallas_call | solution.py:368
  41.1 0.5 collective-permute-start.2
  41.6 0.4 shard_map.150.own_ref
  42.0 0.6 %collective-permute-done.2.other_ref = bf16[32,1536]{1,0:T(8,128)(2,1)S(1)} collective-permute-done((bf16[32,1536]{1,0:T(8,128)(2,1)S(1)}, bf16[32,1536]{1,0:T(8,128)(2,1)S(1)}, u32[]{:S(2)}, u32[]{:S(2)}) %collective-permute-start.2) | collective-permute-done | bytes 98336 | tf_op jit(solution)/shard_map/ppermute | solution.py:52
  42.6 0.1 shard_map.151
  42.6 9.5 %all_to_all.23.parts_ref = bf16[32,3,4,128]{3,2,1,0:T(4,128)(2,1)S(1)} all-to-all(bf16[32,3,4,128]{3,2,1,0:T(4,128)(2,1)S(1)} %shard_map.151), channel_id=1, replica_groups=mesh['group'=1,'wide'=32] {'wide'}, dimensions={0} | all-to-all | bytes 196608 | tf_op jit(solution)/shard_map/all_to_all | solution.py:37
  52.1 0.7 %shard_map.152 = bf16[1,3072]{1,0:T(2,128)(2,1)} custom-call(bf16[32,3,4,128]{3,2,1,0:T(4,128)(2,1)S(1)} %all_to_all.23.parts_ref, f32[24,128]{1,0:T(8,128)S(1)} %get-tuple-element.30.hid_ref), custom_call_target="tpu_custom_call" | custom-call | flops 98304 | bytes 196608 | tf_op jit(solution)/shard_map/pallas_call | solution.py:390
Async XLA Ops:
  0.0 36.7 %copy-start = (bf16[1,576,3072]{2,1,0:T(8,128)(2,1)S(1)}, bf16[1,576,3072]{2,1,0:T(8,128)(2,1)}, u32[]{:S(2)}) copy-start(bf16[1,576,3072]{2,1,0:T(8,128)(2,1)} %param.25) | copy-start | bytes 10616836
  0.0 17.1 %collective-permute-start = (bf16[128,3072]{1,0:T(8,128)(2,1)}, bf16[128,3072]{1,0:T(8,128)(2,1)S(1)}, u32[]{:S(2)}, u32[]{:S(2)}) collective-permute-start(bf16[128,3072]{1,0:T(8,128)(2,1)} %w_out_ref.1), channel_id=1, source_target_pairs={{0,1},{1,0},{2,3},{3,2},{4,5},{5,4},{6,7},{7,6},{8,9},{9,8},{10,11... | collective-permute-start | bytes 2359304 | tf_op jit(solution)/shard_map/ppermute | solution.py:52
  36.6 2.3 %collective-permute-start.1 = (bf16[32,3,4,128]{3,2,1,0:T(4,128)(2,1)S(1)}, bf16[32,3,4,128]{3,2,1,0:T(4,128)(2,1)S(1)}, u32[]{:S(2)}, u32[]{:S(2)}) collective-permute-start(bf16[32,3,4,128]{3,2,1,0:T(4,128)(2,1)S(1)} %all_to_all.22.blocks_ref), channel_id=1, source_target_pairs={{0,1},{1,0},{2,3},{3,2},{4,5},{5,4},{6,7},{7,6},{8,9},{9,8},{10,11... | collective-permute-start | bytes 294920 | tf_op jit(solution)/shard_map/ppermute | solution.py:52
  41.1 1.4 %collective-permute-start.2 = (bf16[32,1536]{1,0:T(8,128)(2,1)S(1)}, bf16[32,1536]{1,0:T(8,128)(2,1)S(1)}, u32[]{:S(2)}, u32[]{:S(2)}) collective-permute-start(bf16[32,1536]{1,0:T(8,128)(2,1)S(1)} %get-tuple-element.29), channel_id=1, source_target_pairs={{0,1},{1,0},{2,3},{3,2},{4,5},{5,4},{6,7},{7,6},{8,9},{9,8},{10,11... | collective-permute-start | bytes 294920 | tf_op jit(solution)/shard_map/ppermute | solution.py:52

commit v4 on v3

--- a/solution.py
+++ b/solution.py
@@ -162,7 +162,7 @@
 
 
 def project(*refs):
-    *column_refs, w_ref, w_other_ref, out_ref, spread = refs
+    *column_refs, w_ref, w_other_ref, _up_ref, _down_ref, out_ref, spread = refs
     rows = out_ref.shape[0]
     if len(column_refs) == 1:
         pair = [column_refs[0][pl.ds(core, rows, stride=2), :] for core in range(2)]
@@ -186,7 +186,7 @@
             held[start : start + size, :] = total[group]
 
 
-def middle(parts_ref, resid_ref, gain_ref, hid_ref, copies_ref, held):
+def middle(parts_ref, resid_ref, gain_ref, _up_ref, _down_ref, hid_ref, copies_ref, held):
     devices, groups, size, _ = copies_ref.shape
     add_up(parts_ref, held)
     hid = (resid_ref[...] + held[...]).astype(jnp.bfloat16).astype(jnp.float32)
@@ -201,44 +201,29 @@
                 copies_ref[at, group] = lines
 
 
-def experts_own(blocks_ref, gate_ref, up_ref, gate_out, up_out, up_own, up_other, spread, inputs, sems):
-    half = up_own.shape[1]
-    copies = []
-    for columns, target in ((own_half(gate_ref), up_own), (other_half(gate_ref), up_other)):
-        copy = pltpu.make_async_copy(up_ref.at[0, :, columns], target, sems.at[len(copies)])
-        copy.start()
-        copies.append(copy)
+def experts_own(blocks_ref, gate_ref, up_ref, gate_out, up_out, spread, inputs):
     given = blocks_to_columns(blocks_ref, spread, inputs)
     gate_out[...] = by_rows(given, gate_ref[:, own_half(gate_ref)])
-    copies[0].wait()
-    up_out[...] = by_rows(given, up_own[...])
-    copies[1].wait()
+    up_out[...] = by_rows(given, up_ref[:, own_half(up_ref)])
 
 
 def experts_other(
-    blocks_ref, gate_ref, up_other, gate_held, up_held, coef_ref, down_ref,
-    inner_ref, send_ref, down_own, down_other, spread, inputs, sems,
+    blocks_ref, gate_ref, up_ref, down_ref, gate_held, up_held, coef_ref,
+    inner_ref, send_ref, spread, inputs,
 ):
-    copies = []
-    for columns, target in ((other_half(gate_ref), down_other), (own_half(gate_ref), down_own)):
-        copy = pltpu.make_async_copy(down_ref.at[0, :, columns], target, sems.at[len(copies)])
-        copy.start()
-        copies.append(copy)
     given = blocks_to_columns(blocks_ref, spread, inputs)
     gate = gate_held[...] + by_rows(given, gate_ref[:, other_half(gate_ref)])
-    upper = up_held[...] + by_rows(given, up_other[...])
+    upper = up_held[...] + by_rows(given, up_ref[:, other_half(up_ref)])
     inner = (jax.nn.silu(gate) * upper).astype(jnp.bfloat16)
     inner_ref[...] = inner
-    copies[0].wait()
-    made = multiply(inner, down_other[...])
+    made = multiply(inner, down_ref[:, other_half(down_ref)])
     coef = coef_ref[...]
     for at in range(0, made.shape[1], LANES):
         send_ref[:, at : at + LANES] = (made[:, at : at + LANES] * coef).astype(send_ref.dtype)
-    copies[1].wait()
-
-
-def experts_last(inner_ref, coef_ref, down_own, out_ref):
-    made = multiply(inner_ref[...], down_own[...])
+
+
+def experts_last(inner_ref, coef_ref, down_ref, out_ref):
+    made = multiply(inner_ref[...], down_ref[:, own_half(down_ref)])
     coef = coef_ref[...]
     for at in range(0, made.shape[1], LANES):
         out_ref[:, at : at + LANES] = made[:, at : at + LANES] * coef
@@ -329,6 +314,7 @@
         )
     )
     w_out_other = swap(w_out)
+    w_gate, w_up, w_down = (w.reshape(w.shape[1:]) for w in (w_gate, w_up, w_down))
     if paired:
         columns = exchange(attn.reshape(devices, 2, LANES))
         columns = [columns.reshape(2 * devices, LANES)]
@@ -339,41 +325,37 @@
     parts = call(
         project,
         blocks,
-        [VMEM] * (2 + len(columns)),
+        [VMEM] * (2 + len(columns)) + [HBM] * 2,
         [spread],
         2 * devices * w_out.size,
         2 * w_out.size,
         4 * MIB,
-    )(*on_chip(*columns, w_out_half, w_out_other))
+    )(*on_chip(*columns, w_out_half, w_out_other), *off_chip(w_up, w_down))
     hid, copies = call(
-        middle, (row, blocks), [VMEM] * 3, [row], devices * width, 4 * devices * width, 2 * MIB
-    )(*on_chip(exchange(parts), resid_rows, moe_rows))
+        middle, (row, blocks), [VMEM] * 5, [row], devices * width, 4 * devices * width, 2 * MIB
+    )(*on_chip(exchange(parts), resid_rows, moe_rows, w_up, w_down))
     given = exchange(copies)
     given_other = swap(given)
     inputs = pltpu.VMEM((devices, half), bf16)
     partial_sum = pltpu.VMEM((devices, hidden), f32)
-    weight = pltpu.VMEM((hidden, half), bf16)
-    gate_weight = w_gate.reshape(w_gate.shape[1:])
-    *sums, up_other = call(
-        lambda blocks_ref, gate_ref, up_ref, gate_out, up_out, up_other, *rest: experts_own(
-            blocks_ref, gate_ref, up_ref, gate_out, up_out, rest[0], up_other, *rest[1:]
-        ),
-        (partial_sum, partial_sum, weight),
-        [VMEM] * 2 + [HBM],
-        [weight, spread, inputs, pltpu.SemaphoreType.DMA((2,))],
+    sums = call(
+        experts_own,
+        (partial_sum, partial_sum),
+        [VMEM] * 3,
+        [spread, inputs],
         2 * devices * hidden * width,
         4 * hidden * width,
         8 * MIB,
-    )(*on_chip(given, gate_weight), *off_chip(w_up))
-    inner, send, down_own = call(
+    )(*on_chip(given, w_gate, w_up))
+    inner, send = call(
         experts_other,
-        (pltpu.VMEM((devices, hidden), bf16), inputs, weight),
-        [VMEM] * 6 + [HBM],
-        [weight, spread, inputs, pltpu.SemaphoreType.DMA((2,))],
+        (pltpu.VMEM((devices, hidden), bf16), inputs),
+        [VMEM] * 7,
+        [spread, inputs],
         3 * devices * hidden * width,
         4 * hidden * width,
         8 * MIB,
-    )(*on_chip(given_other, gate_weight, up_other, *sums, coef), *off_chip(w_down))
+    )(*on_chip(given_other, w_gate, w_up, w_down, *sums, coef))
     received = swap(send)
     own = call(
         experts_last,
@@ -383,7 +365,7 @@
         devices * hidden * width,
         hidden * width,
         4 * MIB,
-    )(*on_chip(inner, coef, down_own))
+    )(*on_chip(inner, coef, w_down))
     outcome = call(
         join, blocks, [VMEM] * 2, [spread], devices * width, 4 * devices * width, 4 * MIB
     )(*on_chip(own, received))

time: 52.9 us -> 51.4 us (0.972)
  Pallas kernels: 8.5 us -> 6.47 us
    pallas_call x4, Pallas kernels: 4.89 us -> 3.09 us  [the longest x1 1.51 us: shards(): call(experts_other, (pltpu.VMEM((devices, hidden), bf16), inputs), [VMEM]...]
  transfers between devices with their start and end apart: 3 -> 3, of which waited for: 1 -> 2; matrix products, arithmetic and copies ran while one was open for 0% -> 0% of each run, Pallas kernels for 10% -> 7%
where the time goes in v4:
time: 51.4 us; the launch traced here: 51.1 us
  blocking collectives  43 us (84%)
  Pallas kernels  6.47 us (13%)
  starting transfers between devices  1.02 us (2%)
  waiting for transfers between devices  0.62 us (1%)
    all_to_all x4, blocking collectives, exchange(): lax.all_to_all(blocks, 'wide', split_axis=0, concat_axis=0, tiled=True)  43 us
    pallas_call x1, Pallas kernels, shards(): call(attention, (pltpu.VMEM((2 * heads if paired else heads, LANES), f32)...  2.27 us
    pallas_call x1, Pallas kernels, shards(): call(experts_other, (pltpu.VMEM((devices, hidden), bf16), inputs), [VMEM]...  1.51 us
    pallas_call x1, Pallas kernels, shards(): call(experts_own, (partial_sum, partial_sum), [VMEM] * 3, [spread, inputs...  1.11 us
  transfers between devices with their start and end apart: 3, of which 2 were waited for; matrix products, arithmetic and copies ran while one was open for 0% of the time, Pallas kernels for 7%

profile of v4, /device:TPU:0, one launch (start us, length us, event | category | flops | bytes accessed | tf_op | source)
XLA Modules:
  0.0 51.1 jit_solution(9657726160221221641)
XLA Ops:
  0.0 0.5 collective-permute-start
  0.5 2.3 %shard_map.145 = (f32[64,128]{1,0:T(8,128)S(1)}, f32[24,128]{1,0:T(8,128)S(1)}, f32[24,128]{1,0:T(8,128)S(1)}, f32[32,128]{1,0:T(8,128)S(1)}, bf16[128,1536]{1,0:T(8,128)(2,1)S(1)}) custom-call(bf16[1,4096]{1,0:T(2,128)(2,1)} %query_ref.1, bf16[1,4096]{1,0:T(2,128)(2,1)} %key_ref.1, bf16[1,4096]{1,0:T(2,128)(2,1)} %value_ref.1, bf16[1,4096]{1,0:T(2,128)(2,1)} %gate_ref.1, ...), custom_call_target="tpu_custom_call" | custom-call | flops 1048576 | bytes 2097152 | tf_op jit(solution)/shard_map/pallas_call | solution.py:276
  2.8 14.0 %all_to_all.20 = f32[32,2,128]{2,1,0:T(2,128)S(1)} all-to-all(f32[32,2,128]{2,1,0:T(2,128)S(1)} %bitcast.20), channel_id=1, replica_groups=mesh['group'=1,'wide'=32] {'wide'}, dimensions={0} | all-to-all | bytes 65536 | tf_op jit(solution)/shard_map/all_to_all | solution.py:37
  16.8 0.0 collective-permute-done.refs_2_
  16.8 0.0 copy-start
  16.8 0.0 copy-start.1
  16.8 0.3 shard_map.146
  17.1 9.7 %all_to_all.21.parts_ref = bf16[32,3,4,128]{3,2,1,0:T(4,128)(2,1)S(1)} all-to-all(bf16[32,3,4,128]{3,2,1,0:T(4,128)(2,1)S(1)} %shard_map.146), channel_id=1, replica_groups=mesh['group'=1,'wide'=32] {'wide'}, dimensions={0} | all-to-all | bytes 196608 | tf_op jit(solution)/shard_map/all_to_all | solution.py:37
  26.8 0.0 copy-done
  26.8 0.0 copy-done.1
  26.8 0.0 copy-start.2
  26.8 0.2 shard_map.147
  27.0 9.7 %all_to_all.22.blocks_ref = bf16[32,3,4,128]{3,2,1,0:T(4,128)(2,1)S(1)} all-to-all(bf16[32,3,4,128]{3,2,1,0:T(4,128)(2,1)S(1)} %get-tuple-element.20), channel_id=1, replica_groups=mesh['group'=1,'wide'=32] {'wide'}, dimensions={0} | all-to-all | bytes 196608 | tf_op jit(solution)/shard_map/all_to_all | solution.py:37
  36.8 0.1 collective-permute-start.1
  36.9 0.0 copy-done.2
  36.9 1.1 %shard_map.148 = (f32[32,576]{1,0:T(8,128)S(1)}, f32[32,576]{1,0:T(8,128)S(1)}) custom-call(bf16[32,3,4,128]{3,2,1,0:T(4,128)(2,1)S(1)} %all_to_all.22.blocks_ref, bf16[576,3072]{1,0:T(8,128)(2,1)S(1)} %bitcast.17, bf16[576,3072]{1,0:T(8,128)(2,1)S(1)} %bitcast.11), custom_call_target="tpu_custom_call" | custom-call | flops 113246208 | bytes 7077888 | tf_op jit(solution)/shard_map/pallas_call | solution.py:341
  38.0 0.1 collective-permute-done.1.blocks_ref
  38.1 1.5 %shard_map.149 = (bf16[32,576]{1,0:T(8,128)(2,1)S(1)}, bf16[32,1536]{1,0:T(8,128)(2,1)S(1)}) custom-call(bf16[32,3,4,128]{3,2,1,0:T(4,128)(2,1)S(1)} %collective-permute-done.1.blocks_ref, bf16[576,3072]{1,0:T(8,128)(2,1)S(1)} %bitcast.18, bf16[576,3072]{1,0:T(8,128)(2,1)S(1)} %bitcast.12, bf16[576,3072]{1,0:T(8,128)(2,1)S(1)} %bitcast.15, ...), custom_call_target="tpu_custom_call" | custom-call | flops 169869312 | bytes 7077888 | tf_op jit(solution)/shard_map/pallas_call | solution.py:350
  39.6 0.4 collective-permute-start.2
  40.0 0.4 shard_map.150.own_ref
  40.4 0.6 %collective-permute-done.2.other_ref = bf16[32,1536]{1,0:T(8,128)(2,1)S(1)} collective-permute-done((bf16[32,1536]{1,0:T(8,128)(2,1)S(1)}, bf16[32,1536]{1,0:T(8,128)(2,1)S(1)}, u32[]{:S(2)}, u32[]{:S(2)}) %collective-permute-start.2) | collective-permute-done | bytes 98336 | tf_op jit(solution)/shard_map/ppermute | solution.py:52
  41.0 0.1 shard_map.151
  41.0 9.5 %all_to_all.23.parts_ref = bf16[32,3,4,128]{3,2,1,0:T(4,128)(2,1)S(1)} all-to-all(bf16[32,3,4,128]{3,2,1,0:T(4,128)(2,1)S(1)} %shard_map.151), channel_id=1, replica_groups=mesh['group'=1,'wide'=32] {'wide'}, dimensions={0} | all-to-all | bytes 196608 | tf_op jit(solution)/shard_map/all_to_all | solution.py:37
  50.5 0.7 %shard_map.152 = bf16[1,3072]{1,0:T(2,128)(2,1)} custom-call(bf16[32,3,4,128]{3,2,1,0:T(4,128)(2,1)S(1)} %all_to_all.23.parts_ref, f32[24,128]{1,0:T(8,128)S(1)} %get-tuple-element.26.hid_ref), custom_call_target="tpu_custom_call" | custom-call | flops 98304 | bytes 196608 | tf_op jit(solution)/shard_map/pallas_call | solution.py:372
Async XLA Ops:
  0.0 16.8 %collective-permute-start = (bf16[128,3072]{1,0:T(8,128)(2,1)}, bf16[128,3072]{1,0:T(8,128)(2,1)S(1)}, u32[]{:S(2)}, u32[]{:S(2)}) collective-permute-start(bf16[128,3072]{1,0:T(8,128)(2,1)} %w_out_ref.1), channel_id=1, source_target_pairs={{0,1},{1,0},{2,3},{3,2},{4,5},{5,4},{6,7},{7,6},{8,9},{9,8},{10,11... | collective-permute-start | bytes 2359304 | tf_op jit(solution)/shard_map/ppermute | solution.py:52
  16.8 10.0 %copy-start = (bf16[1,576,3072]{2,1,0:T(8,128)(2,1)S(1)}, bf16[1,576,3072]{2,1,0:T(8,128)(2,1)}, u32[]{:S(2)}) copy-start(bf16[1,576,3072]{2,1,0:T(8,128)(2,1)} %param.26) | copy-start | bytes 10616836
  16.8 10.0 %copy-start.1 = (bf16[1,576,3072]{2,1,0:T(8,128)(2,1)S(1)}, bf16[1,576,3072]{2,1,0:T(8,128)(2,1)}, u32[]{:S(2)}) copy-start(bf16[1,576,3072]{2,1,0:T(8,128)(2,1)} %param.27) | copy-start | bytes 10616836
  26.8 10.1 %copy-start.2 = (bf16[1,576,3072]{2,1,0:T(8,128)(2,1)S(1)}, bf16[1,576,3072]{2,1,0:T(8,128)(2,1)}, u32[]{:S(2)}) copy-start(bf16[1,576,3072]{2,1,0:T(8,128)(2,1)} %param.25) | copy-start | bytes 10616836
  36.8 1.3 %collective-permute-start.1 = (bf16[32,3,4,128]{3,2,1,0:T(4,128)(2,1)S(1)}, bf16[32,3,4,128]{3,2,1,0:T(4,128)(2,1)S(1)}, u32[]{:S(2)}, u32[]{:S(2)}) collective-permute-start(bf16[32,3,4,128]{3,2,1,0:T(4,128)(2,1)S(1)} %all_to_all.22.blocks_ref), channel_id=1, source_target_pairs={{0,1},{1,0},{2,3},{3,2},{4,5},{5,4},{6,7},{7,6},{8,9},{9,8},{10,11... | collective-permute-start | bytes 294920 | tf_op jit(solution)/shard_map/ppermute | solution.py:52
  39.6 1.4 %collective-permute-start.2 = (bf16[32,1536]{1,0:T(8,128)(2,1)S(1)}, bf16[32,1536]{1,0:T(8,128)(2,1)S(1)}, u32[]{:S(2)}, u32[]{:S(2)}) collective-permute-start(bf16[32,1536]{1,0:T(8,128)(2,1)S(1)} %get-tuple-element.25), channel_id=1, source_target_pairs={{0,1},{1,0},{2,3},{3,2},{4,5},{5,4},{6,7},{7,6},{8,9},{9,8},{10,11... | collective-permute-start | bytes 294920 | tf_op jit(solution)/shard_map/ppermute | solution.py:52

commit v5 on v4

--- a/solution.py
+++ b/solution.py
@@ -53,16 +53,14 @@
 
 
 def unfold(row_ref, held):
-    for at in range(held.shape[0]):
-        held[at : at + 1, :] = row_ref[0:1, at * LANES : (at + 1) * LANES].astype(jnp.float32)
+    held[...] = row_ref[...].astype(jnp.float32).reshape(held.shape)
 
 
 def attention(
-    query_ref, key_ref, value_ref, gate_ref, norm_ref, decay_ref, state_ref, resid_ref,
-    moe_ref, ids_ref, weights_ref, w_out_ref,
-    out_ref, resid_out, moe_out, coef_ref, w_out_half,
-    rows, norm_held, decay_held, states, resid_held, ids_held, weights_held,
-    q_held, k_held, v_held, g_held, att, sems,
+    query_ref, key_ref, value_ref, gate_ref, norm_ref, decay_ref, state_ref,
+    ids_ref, weights_ref, w_out_ref, out_ref, coef_ref, w_out_half,
+    rows, norm_held, decay_held, states, ids_held, weights_held,
+    q_held, k_held, v_held, g_held, att, q_wide, sems,
 ):
     heads = decay_held.shape[0]
     block = heads // HEAD_BLOCKS
@@ -80,10 +78,9 @@
     read = [fetch(state_ref.at[0, part], states.at[part]) for part in parts]
     later = [fetch(ref, rows.at[2 + at]) for at, ref in enumerate((value_ref, gate_ref))]
     later.append(fetch(norm_ref, norm_held))
-    later.append(fetch(resid_ref, resid_held))
     later.append(fetch(ids_ref, ids_held))
     later.append(fetch(weights_ref, weights_held))
-    last = [fetch(moe_ref, moe_out), fetch(w_out_ref.at[:, own_half(w_out_ref)], w_out_half)]
+    last = [fetch(w_out_ref.at[:, own_half(w_out_ref)], w_out_half)]
 
     for copy in small:
         copy.wait()
@@ -92,10 +89,12 @@
     q_rows = q_held[...]
     q_columns = q_rows.T
     both = jnp.sum(q_rows * k_held[...], axis=1, keepdims=True)
+    for head in range(heads):
+        q_wide[head] = jnp.broadcast_to(q_columns[:, head : head + 1], q_wide.shape[1:])
     for at in range(HEAD_BLOCKS):
         read[at].wait()
         for head in range(at * block, (at + 1) * block):
-            seen = jnp.sum(q_columns[:, head : head + 1] * states[head], axis=0, keepdims=True)
+            seen = jnp.sum(q_wide[head] * states[head], axis=0, keepdims=True)
             fade = jnp.exp(jnp.full((1, LANES), -decay_held[head], jnp.float32))
             att[head : head + 1, :] = fade * seen
     for copy in later:
@@ -114,7 +113,6 @@
             out_ref[pl.ds(core, heads // 2, stride=4), :] = of_core
             out_ref[pl.ds(core + 2, heads // 2, stride=4), :] = of_core
 
-    unfold(resid_held, resid_out)
     owner = lax.axis_index("wide") // SPLIT
     named = jnp.where(ids_held[...] == owner, weights_held[...], 0.0)
     along = jnp.sum(named, axis=0, keepdims=True)
@@ -162,7 +160,7 @@
 
 
 def project(*refs):
-    *column_refs, w_ref, w_other_ref, _up_ref, _down_ref, out_ref, spread = refs
+    *column_refs, w_ref, w_other_ref, _up_ref, _down_ref, _gate_ref, out_ref, spread = refs
     rows = out_ref.shape[0]
     if len(column_refs) == 1:
         pair = [column_refs[0][pl.ds(core, rows, stride=2), :] for core in range(2)]
@@ -186,10 +184,11 @@
             held[start : start + size, :] = total[group]
 
 
-def middle(parts_ref, resid_ref, gain_ref, _up_ref, _down_ref, hid_ref, copies_ref, held):
+def middle(parts_ref, resid_ref, gain_ref, _up_ref, _down_ref, _gate_ref, hid_ref, copies_ref, held, resid_rows):
     devices, groups, size, _ = copies_ref.shape
     add_up(parts_ref, held)
-    hid = (resid_ref[...] + held[...]).astype(jnp.bfloat16).astype(jnp.float32)
+    unfold(resid_ref, resid_rows)
+    hid = (resid_rows[...] + held[...]).astype(jnp.bfloat16).astype(jnp.float32)
     hid_ref[...] = hid
     scale = lax.rsqrt(jnp.sum(hid * hid, keepdims=True) / hid.size + 1e-06)
     held[...] = hid * scale * gain_ref[...]
@@ -273,27 +272,25 @@
     per_head = pltpu.VMEM((heads, LANES), f32)
     paired = each == LANES
 
-    attn, resid_rows, moe_rows, coef, w_out_half = call(
+    attn, coef, w_out_half = call(
         attention,
         (
             pltpu.VMEM((2 * heads if paired else heads, LANES), f32),
-            row,
-            row,
             pltpu.VMEM((devices, LANES), f32),
             pltpu.VMEM((each, half), bf16),
         ),
-        [HBM] * 12,
+        [HBM] * 10,
         [
             pltpu.VMEM((4, 1, features), bf16),
             per_head,
             pltpu.SMEM((heads,), f32),
             pltpu.VMEM(state.shape[1:], f32),
-            pltpu.VMEM((1, width), bf16),
             pltpu.VMEM((2, devices), jnp.int32),
             pltpu.VMEM((2, devices), f32),
         ]
         + [per_head] * 5
-        + [pltpu.SemaphoreType.DMA((11 + HEAD_BLOCKS,))],
+        + [pltpu.VMEM(state.shape[1:], f32)]
+        + [pltpu.SemaphoreType.DMA((9 + HEAD_BLOCKS,))],
         2 * state.size,
         4 * state.size,
         8 * MIB,
@@ -306,8 +303,6 @@
             norm_gain.reshape(heads, LANES),
             decay,
             state,
-            resid,
-            moe_gain.reshape(tiles, LANES),
             expert_ids.T,
             expert_weights.T,
             w_out,
@@ -325,15 +320,15 @@
     parts = call(
         project,
         blocks,
-        [VMEM] * (2 + len(columns)) + [HBM] * 2,
+        [VMEM] * (2 + len(columns)) + [HBM] * 3,
         [spread],
         2 * devices * w_out.size,
         2 * w_out.size,
         4 * MIB,
-    )(*on_chip(*columns, w_out_half, w_out_other), *off_chip(w_up, w_down))
+    )(*on_chip(*columns, w_out_half, w_out_other), *off_chip(w_up, w_down, w_gate))
     hid, copies = call(
-        middle, (row, blocks), [VMEM] * 5, [row], devices * width, 4 * devices * width, 2 * MIB
-    )(*on_chip(exchange(parts), resid_rows, moe_rows, w_up, w_down))
+        middle, (row, blocks), [VMEM] * 6, [row, row], devices * width, 4 * devices * width, 2 * MIB
+    )(*on_chip(exchange(parts), resid, moe_gain.reshape(tiles, LANES), w_up, w_down, w_gate))
     given = exchange(copies)
     given_other = swap(given)
     inputs = pltpu.VMEM((devices, half), bf16)

time: 51.4 us -> 51 us (level)
  no operation moved by 1% of the time
where the time goes in v5:
time: 51 us; the launch traced here: 50.8 us
  blocking collectives  42.7 us (84%)
  Pallas kernels  6.28 us (12%)
  starting transfers between devices  1.01 us (2%)
  waiting for transfers between devices  0.65 us (1%)
    all_to_all x4, blocking collectives, exchange(): lax.all_to_all(blocks, 'wide', split_axis=0, concat_axis=0, tiled=True)  42.7 us
    pallas_call x1, Pallas kernels, shards(): call(attention, (pltpu.VMEM((2 * heads if paired else heads, LANES), f32)...  2.08 us
    pallas_call x1, Pallas kernels, shards(): call(experts_other, (pltpu.VMEM((devices, hidden), bf16), inputs), [VMEM]...  1.52 us
    pallas_call x1, Pallas kernels, shards(): call(experts_own, (partial_sum, partial_sum), [VMEM] * 3, [spread, inputs...  1.11 us
  transfers between devices with their start and end apart: 3, of which 2 were waited for; matrix products, arithmetic and copies ran while one was open for 0% of the time, Pallas kernels for 7%

profile of v5, /device:TPU:0, one launch (start us, length us, event | category | flops | bytes accessed | tf_op | source)
XLA Modules:
  0.0 50.8 jit_solution(14205173382067451742)
XLA Ops:
  0.0 0.5 collective-permute-start
  0.5 2.1 %shard_map.145 = (f32[64,128]{1,0:T(8,128)S(1)}, f32[32,128]{1,0:T(8,128)S(1)}, bf16[128,1536]{1,0:T(8,128)(2,1)S(1)}) custom-call(bf16[1,4096]{1,0:T(2,128)(2,1)} %query_ref.1, bf16[1,4096]{1,0:T(2,128)(2,1)} %key_ref.1, bf16[1,4096]{1,0:T(2,128)(2,1)} %value_ref.1, bf16[1,4096]{1,0:T(2,128)(2,1)} %gate_ref.1, f32[32,128]{1,0:T(8,128)} %bitcast.24, ...), custom_call_target="tpu_custom_call" | custom-call | flops 1048576 | bytes 2097152 | tf_op jit(solution)/shard_map/pallas_call | solution.py:275
  2.6 14.0 %all_to_all.20 = f32[32,2,128]{2,1,0:T(2,128)S(1)} all-to-all(f32[32,2,128]{2,1,0:T(2,128)S(1)} %bitcast.22), channel_id=1, replica_groups=mesh['group'=1,'wide'=32] {'wide'}, dimensions={0} | all-to-all | bytes 65536 | tf_op jit(solution)/shard_map/all_to_all | solution.py:37
  16.6 0.0 collective-permute-done.refs_2_
  16.6 0.0 copy-start
  16.6 0.0 copy-start.1
  16.6 0.0 copy-start.2
  16.6 0.0 copy-start.3
  16.6 0.0 copy-start.4
  16.6 0.3 shard_map.146
  16.9 9.7 %all_to_all.21.parts_ref = bf16[32,3,4,128]{3,2,1,0:T(4,128)(2,1)S(1)} all-to-all(bf16[32,3,4,128]{3,2,1,0:T(4,128)(2,1)S(1)} %shard_map.146), channel_id=1, replica_groups=mesh['group'=1,'wide'=32] {'wide'}, dimensions={0} | all-to-all | bytes 196608 | tf_op jit(solution)/shard_map/all_to_all | solution.py:37
  26.7 0.0 copy-done
  26.7 0.0 copy-done.1
  26.7 0.0 copy-done.2
  26.7 0.0 copy-done.3
  26.7 0.0 copy-done.4
  26.7 0.2 shard_map.147
  26.9 9.5 %all_to_all.22.blocks_ref = bf16[32,3,4,128]{3,2,1,0:T(4,128)(2,1)S(1)} all-to-all(bf16[32,3,4,128]{3,2,1,0:T(4,128)(2,1)S(1)} %get-tuple-element.16), channel_id=1, replica_groups=mesh['group'=1,'wide'=32] {'wide'}, dimensions={0} | all-to-all | bytes 196608 | tf_op jit(solution)/shard_map/all_to_all | solution.py:37
  36.4 0.1 collective-permute-start.1
  36.5 1.1 %shard_map.148 = (f32[32,576]{1,0:T(8,128)S(1)}, f32[32,576]{1,0:T(8,128)S(1)}) custom-call(bf16[32,3,4,128]{3,2,1,0:T(4,128)(2,1)S(1)} %all_to_all.22.blocks_ref, bf16[576,3072]{1,0:T(8,128)(2,1)S(1)} %bitcast.15, bf16[576,3072]{1,0:T(8,128)(2,1)S(1)} %bitcast.11), custom_call_target="tpu_custom_call" | custom-call | flops 113246208 | bytes 7077888 | tf_op jit(solution)/shard_map/pallas_call | solution.py:336
  37.6 0.1 collective-permute-done.1.blocks_ref
  37.7 1.5 %shard_map.149 = (bf16[32,576]{1,0:T(8,128)(2,1)S(1)}, bf16[32,1536]{1,0:T(8,128)(2,1)S(1)}) custom-call(bf16[32,3,4,128]{3,2,1,0:T(4,128)(2,1)S(1)} %collective-permute-done.1.blocks_ref, bf16[576,3072]{1,0:T(8,128)(2,1)S(1)} %bitcast.16, bf16[576,3072]{1,0:T(8,128)(2,1)S(1)} %bitcast.12, bf16[576,3072]{1,0:T(8,128)(2,1)S(1)} %bitcast.19, ...), custom_call_target="tpu_custom_call" | custom-call | flops 169869312 | bytes 7077888 | tf_op jit(solution)/shard_map/pallas_call | solution.py:345
  39.2 0.4 collective-permute-start.2
  39.6 0.4 shard_map.150.own_ref
  40.0 0.6 %collective-permute-done.2.other_ref = bf16[32,1536]{1,0:T(8,128)(2,1)S(1)} collective-permute-done((bf16[32,1536]{1,0:T(8,128)(2,1)S(1)}, bf16[32,1536]{1,0:T(8,128)(2,1)S(1)}, u32[]{:S(2)}, u32[]{:S(2)}) %collective-permute-start.2) | collective-permute-done | bytes 98336 | tf_op jit(solution)/shard_map/ppermute | solution.py:52
  40.6 0.1 shard_map.151
  40.6 9.5 %all_to_all.23.parts_ref = bf16[32,3,4,128]{3,2,1,0:T(4,128)(2,1)S(1)} all-to-all(bf16[32,3,4,128]{3,2,1,0:T(4,128)(2,1)S(1)} %shard_map.151), channel_id=1, replica_groups=mesh['group'=1,'wide'=32] {'wide'}, dimensions={0} | all-to-all | bytes 196608 | tf_op jit(solution)/shard_map/all_to_all | solution.py:37
  50.1 0.7 %shard_map.152 = bf16[1,3072]{1,0:T(2,128)(2,1)} custom-call(bf16[32,3,4,128]{3,2,1,0:T(4,128)(2,1)S(1)} %all_to_all.23.parts_ref, f32[24,128]{1,0:T(8,128)S(1)} %get-tuple-element.22.hid_ref), custom_call_target="tpu_custom_call" | custom-call | flops 98304 | bytes 196608 | tf_op jit(solution)/shard_map/pallas_call | solution.py:367
Async XLA Ops:
  0.0 16.6 %collective-permute-start = (bf16[128,3072]{1,0:T(8,128)(2,1)}, bf16[128,3072]{1,0:T(8,128)(2,1)S(1)}, u32[]{:S(2)}, u32[]{:S(2)}) collective-permute-start(bf16[128,3072]{1,0:T(8,128)(2,1)} %w_out_ref.1), channel_id=1, source_target_pairs={{0,1},{1,0},{2,3},{3,2},{4,5},{5,4},{6,7},{7,6},{8,9},{9,8},{10,11... | collective-permute-start | bytes 2359304 | tf_op jit(solution)/shard_map/ppermute | solution.py:52
  16.6 10.1 %copy-start = (bf16[1,576,3072]{2,1,0:T(8,128)(2,1)S(1)}, bf16[1,576,3072]{2,1,0:T(8,128)(2,1)}, u32[]{:S(2)}) copy-start(bf16[1,576,3072]{2,1,0:T(8,128)(2,1)} %param.26) | copy-start | bytes 10616836
  16.6 10.1 %copy-start.1 = (bf16[1,576,3072]{2,1,0:T(8,128)(2,1)S(1)}, bf16[1,576,3072]{2,1,0:T(8,128)(2,1)}, u32[]{:S(2)}) copy-start(bf16[1,576,3072]{2,1,0:T(8,128)(2,1)} %param.25) | copy-start | bytes 10616836
  16.6 10.1 %copy-start.2 = (bf16[1,576,3072]{2,1,0:T(8,128)(2,1)S(1)}, bf16[1,576,3072]{2,1,0:T(8,128)(2,1)}, u32[]{:S(2)}) copy-start(bf16[1,576,3072]{2,1,0:T(8,128)(2,1)} %param.27) | copy-start | bytes 10616836
  16.6 10.1 %copy-start.3 = (bf16[1,3072]{1,0:T(2,128)(2,1)S(1)}, bf16[1,3072]{1,0:T(2,128)(2,1)}, u32[]{:S(2)}) copy-start(bf16[1,3072]{1,0:T(2,128)(2,1)} %resid_ref.1) | copy-start | bytes 18436
  16.6 10.1 %copy-start.4 = (f32[3072]{0:T(1024)S(1)}, f32[3072]{0:T(1024)}, u32[]{:S(2)}) copy-start(f32[3072]{0:T(1024)} %param.24) | copy-start | bytes 36868
  36.4 1.3 %collective-permute-start.1 = (bf16[32,3,4,128]{3,2,1,0:T(4,128)(2,1)S(1)}, bf16[32,3,4,128]{3,2,1,0:T(4,128)(2,1)S(1)}, u32[]{:S(2)}, u32[]{:S(2)}) collective-permute-start(bf16[32,3,4,128]{3,2,1,0:T(4,128)(2,1)S(1)} %all_to_all.22.blocks_ref), channel_id=1, source_target_pairs={{0,1},{1,0},{2,3},{3,2},{4,5},{5,4},{6,7},{7,6},{8,9},{9,8},{10,11... | collective-permute-start | bytes 294920 | tf_op jit(solution)/shard_map/ppermute | solution.py:52
  39.2 1.4 %collective-permute-start.2 = (bf16[32,1536]{1,0:T(8,128)(2,1)S(1)}, bf16[32,1536]{1,0:T(8,128)(2,1)S(1)}, u32[]{:S(2)}, u32[]{:S(2)}) collective-permute-start(bf16[32,1536]{1,0:T(8,128)(2,1)S(1)} %get-tuple-element.21), channel_id=1, source_target_pairs={{0,1},{1,0},{2,3},{3,2},{4,5},{5,4},{6,7},{7,6},{8,9},{9,8},{10,11... | collective-permute-start | bytes 294920 | tf_op jit(solution)/shard_map/ppermute | solution.py:52

commit v6 on v5

--- a/solution.py
+++ b/solution.py
@@ -103,15 +103,7 @@
     unfold(rows.at[3], g_held)
     found = att[...] + both * v_held[...]
     scale = lax.rsqrt(jnp.sum(found * found, keepdims=True) / found.size + 1e-06)
-    made = found * scale * norm_held[...] * jax.nn.sigmoid(g_held[...])
-    if out_ref.shape[0] == heads:
-        out_ref[...] = made
-    else:
-        att[...] = made
-        for core in range(2):
-            of_core = att[pl.ds(core, heads // 2, stride=2), :]
-            out_ref[pl.ds(core, heads // 2, stride=4), :] = of_core
-            out_ref[pl.ds(core + 2, heads // 2, stride=4), :] = of_core
+    out_ref[...] = found * scale * norm_held[...] * jax.nn.sigmoid(g_held[...])
 
     owner = lax.axis_index("wide") // SPLIT
     named = jnp.where(ids_held[...] == owner, weights_held[...], 0.0)
@@ -122,6 +114,17 @@
     coef_ref[...] = jnp.broadcast_to(column, coef_ref.shape)
     for copy in last:
         copy.wait()
+
+
+def pair_up(rows_ref, _gate_ref, _up_ref, _down_ref, out_ref):
+    heads = rows_ref.shape[0]
+    if out_ref.shape[0] == heads:
+        out_ref[...] = rows_ref[...]
+        return
+    for core in range(2):
+        of_core = rows_ref[pl.ds(core, heads // 2, stride=2), :]
+        out_ref[pl.ds(core, heads // 2, stride=4), :] = of_core
+        out_ref[pl.ds(core + 2, heads // 2, stride=4), :] = of_core
 
 
 def columns_to_blocks(made, spread, out_ref):
@@ -275,7 +278,7 @@
     attn, coef, w_out_half = call(
         attention,
         (
-            pltpu.VMEM((2 * heads if paired else heads, LANES), f32),
+            per_head,
             pltpu.VMEM((devices, LANES), f32),
             pltpu.VMEM((each, half), bf16),
         ),
@@ -310,6 +313,15 @@
     )
     w_out_other = swap(w_out)
     w_gate, w_up, w_down = (w.reshape(w.shape[1:]) for w in (w_gate, w_up, w_down))
+    attn = call(
+        pair_up,
+        pltpu.VMEM((2 * heads if paired else heads, LANES), f32),
+        [VMEM] + [HBM] * 3,
+        [],
+        heads * LANES,
+        8 * heads * LANES,
+        2 * MIB,
+    )(*on_chip(attn), *off_chip(w_gate, w_up, w_down))
     if paired:
         columns = exchange(attn.reshape(devices, 2, LANES))
         columns = [columns.reshape(2 * devices, LANES)]
@@ -320,12 +332,12 @@
     parts = call(
         project,
         blocks,
-        [VMEM] * (2 + len(columns)) + [HBM] * 3,
+        [VMEM] * (5 + len(columns)),
         [spread],
         2 * devices * w_out.size,
         2 * w_out.size,
         4 * MIB,
-    )(*on_chip(*columns, w_out_half, w_out_other), *off_chip(w_up, w_down, w_gate))
+    )(*on_chip(*columns, w_out_half, w_out_other, w_up, w_down, w_gate))
     hid, copies = call(
         middle, (row, blocks), [VMEM] * 6, [row, row], devices * width, 4 * devices * width, 2 * MIB
     )(*on_chip(exchange(parts), resid, moe_gain.reshape(tiles, LANES), w_up, w_down, w_gate))

time: 51 us -> 50.8 us (level)
    pallas_call x2 -> x3, Pallas kernels: 2.35 us -> 2.35 us  [the longest x1 2.08 us: shards(): call(attention, (per_head, pltpu.VMEM((devices, LANES), f32), pltpu.VMEM(...]
where the time goes in v6:
time: 50.8 us; the launch traced here: 50.5 us
  blocking collectives  42.5 us (84%)
  Pallas kernels  6.28 us (12%)
  starting transfers between devices  1.02 us (2%)
  waiting for transfers between devices  0.63 us (1%)
    all_to_all x4, blocking collectives, exchange(): lax.all_to_all(blocks, 'wide', split_axis=0, concat_axis=0, tiled=True)  42.5 us
    pallas_call x1, Pallas kernels, shards(): call(attention, (per_head, pltpu.VMEM((devices, LANES), f32), pltpu.VMEM(...  2.08 us
    pallas_call x1, Pallas kernels, shards(): call(experts_other, (pltpu.VMEM((devices, hidden), bf16), inputs), [VMEM]...  1.51 us
    pallas_call x1, Pallas kernels, shards(): call(experts_own, (partial_sum, partial_sum), [VMEM] * 3, [spread, inputs...  1.11 us
  transfers between devices with their start and end apart: 3, of which 2 were waited for; matrix products, arithmetic and copies ran while one was open for 0% of the time, Pallas kernels for 7%

profile of v6, /device:TPU:0, one launch (start us, length us, event | category | flops | bytes accessed | tf_op | source)
XLA Modules:
  0.0 50.5 jit_solution(15373556680444790529)
XLA Ops:
  0.0 0.5 collective-permute-start
  0.5 2.1 %shard_map.145 = (f32[32,128]{1,0:T(8,128)S(1)}, f32[32,128]{1,0:T(8,128)S(1)}, bf16[128,1536]{1,0:T(8,128)(2,1)S(1)}) custom-call(bf16[1,4096]{1,0:T(2,128)(2,1)} %query_ref.1, bf16[1,4096]{1,0:T(2,128)(2,1)} %key_ref.1, bf16[1,4096]{1,0:T(2,128)(2,1)} %value_ref.1, bf16[1,4096]{1,0:T(2,128)(2,1)} %gate_ref.1, f32[32,128]{1,0:T(8,128)} %bitcast.27, ...), custom_call_target="tpu_custom_call" | custom-call | flops 1048576 | bytes 2097152 | tf_op jit(solution)/shard_map/pallas_call | solution.py:278
  2.6 0.0 copy-start
  2.6 0.0 copy-start.1
  2.6 0.0 copy-start.2
  2.6 14.0 %all_to_all.20 = f32[32,2,128]{2,1,0:T(2,128)S(1)} all-to-all(f32[32,2,128]{2,1,0:T(2,128)S(1)} %bitcast.25), channel_id=1, replica_groups=mesh['group'=1,'wide'=32] {'wide'}, dimensions={0} | all-to-all | bytes 65536 | tf_op jit(solution)/shard_map/all_to_all | solution.py:37
  16.6 0.0 collective-permute-done.refs_2_
  16.6 0.0 copy-done
  16.6 0.0 copy-done.1
  16.6 0.0 copy-done.2
  16.7 0.0 copy-start.3
  16.7 0.0 copy-start.4
  16.7 0.3 shard_map.147
  17.0 9.5 %all_to_all.21.parts_ref = bf16[32,3,4,128]{3,2,1,0:T(4,128)(2,1)S(1)} all-to-all(bf16[32,3,4,128]{3,2,1,0:T(4,128)(2,1)S(1)} %shard_map.147), channel_id=1, replica_groups=mesh['group'=1,'wide'=32] {'wide'}, dimensions={0} | all-to-all | bytes 196608 | tf_op jit(solution)/shard_map/all_to_all | solution.py:37
  26.4 0.0 copy-done.3
  26.4 0.0 copy-done.4
  26.4 0.2 shard_map.148
  26.7 9.5 %all_to_all.22.blocks_ref = bf16[32,3,4,128]{3,2,1,0:T(4,128)(2,1)S(1)} all-to-all(bf16[32,3,4,128]{3,2,1,0:T(4,128)(2,1)S(1)} %get-tuple-element.16), channel_id=1, replica_groups=mesh['group'=1,'wide'=32] {'wide'}, dimensions={0} | all-to-all | bytes 196608 | tf_op jit(solution)/shard_map/all_to_all | solution.py:37
  36.1 0.1 collective-permute-start.1
  36.3 1.1 %shard_map.149 = (f32[32,576]{1,0:T(8,128)S(1)}, f32[32,576]{1,0:T(8,128)S(1)}) custom-call(bf16[32,3,4,128]{3,2,1,0:T(4,128)(2,1)S(1)} %all_to_all.22.blocks_ref, bf16[576,3072]{1,0:T(8,128)(2,1)S(1)} %bitcast.12, bf16[576,3072]{1,0:T(8,128)(2,1)S(1)} %bitcast.17), custom_call_target="tpu_custom_call" | custom-call | flops 113246208 | bytes 7077888 | tf_op jit(solution)/shard_map/pallas_call | solution.py:348
  37.4 0.1 collective-permute-done.1.blocks_ref
  37.4 1.5 %shard_map.150 = (bf16[32,576]{1,0:T(8,128)(2,1)S(1)}, bf16[32,1536]{1,0:T(8,128)(2,1)S(1)}) custom-call(bf16[32,3,4,128]{3,2,1,0:T(4,128)(2,1)S(1)} %collective-permute-done.1.blocks_ref, bf16[576,3072]{1,0:T(8,128)(2,1)S(1)} %bitcast.13, bf16[576,3072]{1,0:T(8,128)(2,1)S(1)} %bitcast.18, bf16[576,3072]{1,0:T(8,128)(2,1)S(1)} %bitcast.22, ...), custom_call_target="tpu_custom_call" | custom-call | flops 169869312 | bytes 7077888 | tf_op jit(solution)/shard_map/pallas_call | solution.py:357
  39.0 0.4 collective-permute-start.2
  39.4 0.4 shard_map.151.own_ref
  39.8 0.6 %collective-permute-done.2.other_ref = bf16[32,1536]{1,0:T(8,128)(2,1)S(1)} collective-permute-done((bf16[32,1536]{1,0:T(8,128)(2,1)S(1)}, bf16[32,1536]{1,0:T(8,128)(2,1)S(1)}, u32[]{:S(2)}, u32[]{:S(2)}) %collective-permute-start.2) | collective-permute-done | bytes 98336 | tf_op jit(solution)/shard_map/ppermute | solution.py:52
  40.3 0.1 shard_map.152
  40.4 9.5 %all_to_all.23.parts_ref = bf16[32,3,4,128]{3,2,1,0:T(4,128)(2,1)S(1)} all-to-all(bf16[32,3,4,128]{3,2,1,0:T(4,128)(2,1)S(1)} %shard_map.152), channel_id=1, replica_groups=mesh['group'=1,'wide'=32] {'wide'}, dimensions={0} | all-to-all | bytes 196608 | tf_op jit(solution)/shard_map/all_to_all | solution.py:37
  49.9 0.7 %shard_map.153 = bf16[1,3072]{1,0:T(2,128)(2,1)} custom-call(bf16[32,3,4,128]{3,2,1,0:T(4,128)(2,1)S(1)} %all_to_all.23.parts_ref, f32[24,128]{1,0:T(8,128)S(1)} %get-tuple-element.22.hid_ref), custom_call_target="tpu_custom_call" | custom-call | flops 98304 | bytes 196608 | tf_op jit(solution)/shard_map/pallas_call | solution.py:379
  (1 shorter events, 0.0 us)
Async XLA Ops:
  0.0 16.6 %collective-permute-start = (bf16[128,3072]{1,0:T(8,128)(2,1)}, bf16[128,3072]{1,0:T(8,128)(2,1)S(1)}, u32[]{:S(2)}, u32[]{:S(2)}) collective-permute-start(bf16[128,3072]{1,0:T(8,128)(2,1)} %w_out_ref.1), channel_id=1, source_target_pairs={{0,1},{1,0},{2,3},{3,2},{4,5},{5,4},{6,7},{7,6},{8,9},{9,8},{10,11... | collective-permute-start | bytes 2359304 | tf_op jit(solution)/shard_map/ppermute | solution.py:52
  2.6 14.1 %copy-start = (bf16[1,576,3072]{2,1,0:T(8,128)(2,1)S(1)}, bf16[1,576,3072]{2,1,0:T(8,128)(2,1)}, u32[]{:S(2)}) copy-start(bf16[1,576,3072]{2,1,0:T(8,128)(2,1)} %param.25) | copy-start | bytes 10616836
  2.6 14.1 %copy-start.1 = (bf16[1,576,3072]{2,1,0:T(8,128)(2,1)S(1)}, bf16[1,576,3072]{2,1,0:T(8,128)(2,1)}, u32[]{:S(2)}) copy-start(bf16[1,576,3072]{2,1,0:T(8,128)(2,1)} %param.26) | copy-start | bytes 10616836
  2.6 14.0 %copy-start.2 = (bf16[1,576,3072]{2,1,0:T(8,128)(2,1)S(1)}, bf16[1,576,3072]{2,1,0:T(8,128)(2,1)}, u32[]{:S(2)}) copy-start(bf16[1,576,3072]{2,1,0:T(8,128)(2,1)} %param.27) | copy-start | bytes 10616836
  16.7 9.8 %copy-start.3 = (bf16[1,3072]{1,0:T(2,128)(2,1)S(1)}, bf16[1,3072]{1,0:T(2,128)(2,1)}, u32[]{:S(2)}) copy-start(bf16[1,3072]{1,0:T(2,128)(2,1)} %resid_ref.1) | copy-start | bytes 18436
  16.7 9.8 %copy-start.4 = (f32[3072]{0:T(1024)S(1)}, f32[3072]{0:T(1024)}, u32[]{:S(2)}) copy-start(f32[3072]{0:T(1024)} %param.24) | copy-start | bytes 36868
  36.1 1.3 %collective-permute-start.1 = (bf16[32,3,4,128]{3,2,1,0:T(4,128)(2,1)S(1)}, bf16[32,3,4,128]{3,2,1,0:T(4,128)(2,1)S(1)}, u32[]{:S(2)}, u32[]{:S(2)}) collective-permute-start(bf16[32,3,4,128]{3,2,1,0:T(4,128)(2,1)S(1)} %all_to_all.22.blocks_ref), channel_id=1, source_target_pairs={{0,1},{1,0},{2,3},{3,2},{4,5},{5,4},{6,7},{7,6},{8,9},{9,8},{10,11... | collective-permute-start | bytes 294920 | tf_op jit(solution)/shard_map/ppermute | solution.py:52
  39.0 1.4 %collective-permute-start.2 = (bf16[32,1536]{1,0:T(8,128)(2,1)S(1)}, bf16[32,1536]{1,0:T(8,128)(2,1)S(1)}, u32[]{:S(2)}, u32[]{:S(2)}) collective-permute-start(bf16[32,1536]{1,0:T(8,128)(2,1)S(1)} %get-tuple-element.21), channel_id=1, source_target_pairs={{0,1},{1,0},{2,3},{3,2},{4,5},{5,4},{6,7},{7,6},{8,9},{9,8},{10,11... | collective-permute-start | bytes 294920 | tf_op jit(solution)/shard_map/ppermute | solution.py:52

commit v7 on v6

--- a/solution.py
+++ b/solution.py
@@ -58,7 +58,7 @@
 
 def attention(
     query_ref, key_ref, value_ref, gate_ref, norm_ref, decay_ref, state_ref,
-    ids_ref, weights_ref, w_out_ref, out_ref, coef_ref, w_out_half,
+    ids_ref, weights_ref, out_ref, coef_ref,
     rows, norm_held, decay_held, states, ids_held, weights_held,
     q_held, k_held, v_held, g_held, att, q_wide, sems,
 ):
@@ -80,7 +80,6 @@
     later.append(fetch(norm_ref, norm_held))
     later.append(fetch(ids_ref, ids_held))
     later.append(fetch(weights_ref, weights_held))
-    last = [fetch(w_out_ref.at[:, own_half(w_out_ref)], w_out_half)]
 
     for copy in small:
         copy.wait()
@@ -112,11 +111,9 @@
     same = lax.broadcasted_iota(jnp.int32, square, 0) == lax.broadcasted_iota(jnp.int32, square, 1)
     column = jnp.sum(jnp.where(same, along, 0.0), axis=1, keepdims=True)
     coef_ref[...] = jnp.broadcast_to(column, coef_ref.shape)
-    for copy in last:
-        copy.wait()
-
-
-def pair_up(rows_ref, _gate_ref, _up_ref, _down_ref, out_ref):
+
+
+def pair_up(rows_ref, _out_ref, _gate_ref, _up_ref, _down_ref, out_ref):
     heads = rows_ref.shape[0]
     if out_ref.shape[0] == heads:
         out_ref[...] = rows_ref[...]
@@ -172,7 +169,7 @@
     first = lax.rem(lax.axis_index("wide"), 2) == 0
     own = jnp.where(first, pair[0], pair[1]).astype(jnp.bfloat16)
     other = jnp.where(first, pair[1], pair[0]).astype(jnp.bfloat16)
-    made = multiply(own, w_ref[...]) + multiply(other, w_other_ref[:, own_half(w_other_ref)])
+    made = multiply(own, w_ref[:, own_half(w_ref)]) + multiply(other, w_other_ref[:, own_half(w_other_ref)])
     columns_to_blocks(made, spread, out_ref)
 
 
@@ -275,14 +272,13 @@
     per_head = pltpu.VMEM((heads, LANES), f32)
     paired = each == LANES
 
-    attn, coef, w_out_half = call(
+    attn, coef = call(
         attention,
         (
             per_head,
             pltpu.VMEM((devices, LANES), f32),
-            pltpu.VMEM((each, half), bf16),
         ),
-        [HBM] * 10,
+        [HBM] * 9,
         [
             pltpu.VMEM((4, 1, features), bf16),
             per_head,
@@ -293,7 +289,7 @@
         ]
         + [per_head] * 5
         + [pltpu.VMEM(state.shape[1:], f32)]
-        + [pltpu.SemaphoreType.DMA((9 + HEAD_BLOCKS,))],
+        + [pltpu.SemaphoreType.DMA((8 + HEAD_BLOCKS,))],
         2 * state.size,
         4 * state.size,
         8 * MIB,
@@ -308,7 +304,6 @@
             state,
             expert_ids.T,
             expert_weights.T,
-            w_out,
         )
     )
     w_out_other = swap(w_out)
@@ -316,12 +311,12 @@
     attn = call(
         pair_up,
         pltpu.VMEM((2 * heads if paired else heads, LANES), f32),
-        [VMEM] + [HBM] * 3,
+        [VMEM] + [HBM] * 4,
         [],
         heads * LANES,
         8 * heads * LANES,
         2 * MIB,
-    )(*on_chip(attn), *off_chip(w_gate, w_up, w_down))
+    )(*on_chip(attn), *off_chip(w_out, w_gate, w_up, w_down))
     if paired:
         columns = exchange(attn.reshape(devices, 2, LANES))
         columns = [columns.reshape(2 * devices, LANES)]
@@ -337,7 +332,7 @@
         2 * devices * w_out.size,
         2 * w_out.size,
         4 * MIB,
-    )(*on_chip(*columns, w_out_half, w_out_other, w_up, w_down, w_gate))
+    )(*on_chip(*columns, w_out, w_out_other, w_up, w_down, w_gate))
     hid, copies = call(
         middle, (row, blocks), [VMEM] * 6, [row, row], devices * width, 4 * devices * width, 2 * MIB
     )(*on_chip(exchange(parts), resid, moe_gain.reshape(tiles, LANES), w_up, w_down, w_gate))

time: 50.8 us -> 50.8 us (level)
  no operation moved by 1% of the time
where the time goes in v7:
time: 50.8 us; the launch traced here: 50.5 us
  blocking collectives  42.5 us (84%)
  Pallas kernels  6.27 us (12%)
  starting transfers between devices  1.01 us (2%)
  waiting for transfers between devices  0.63 us (1%)
    all_to_all x4, blocking collectives, exchange(): lax.all_to_all(blocks, 'wide', split_axis=0, concat_axis=0, tiled=True)  42.5 us
    pallas_call x1, Pallas kernels, shards(): call(attention, (per_head, pltpu.VMEM((devices, LANES), f32)), [HBM] * 9,...  2.07 us
    pallas_call x1, Pallas kernels, shards(): call(experts_other, (pltpu.VMEM((devices, hidden), bf16), inputs), [VMEM]...  1.52 us
    pallas_call x1, Pallas kernels, shards(): call(experts_own, (partial_sum, partial_sum), [VMEM] * 3, [spread, inputs...  1.11 us
  transfers between devices with their start and end apart: 3, of which 2 were waited for; matrix products, arithmetic and copies ran while one was open for 0% of the time, Pallas kernels for 7%

profile of v7, /device:TPU:0, one launch (start us, length us, event | category | flops | bytes accessed | tf_op | source)
XLA Modules:
  0.0 50.5 jit_solution(13539176655392813205)
XLA Ops:
  0.0 0.5 collective-permute-start
  0.5 2.1 %shard_map.145 = (f32[32,128]{1,0:T(8,128)S(1)}, f32[32,128]{1,0:T(8,128)S(1)}) custom-call(bf16[1,4096]{1,0:T(2,128)(2,1)} %query_ref.1, bf16[1,4096]{1,0:T(2,128)(2,1)} %key_ref.1, bf16[1,4096]{1,0:T(2,128)(2,1)} %value_ref.1, bf16[1,4096]{1,0:T(2,128)(2,1)} %gate_ref.1, f32[32,128]{1,0:T(8,128)} %bitcast.27, f32[32]{0:T(128)} %decay_ref.1, ...), custom_call_target="tpu_custom_call" | custom-call | flops 1048576 | bytes 2097152 | tf_op jit(solution)/shard_map/pallas_call | solution.py:275
  2.6 0.0 copy-start
  2.6 0.0 copy-start.1
  2.6 0.0 copy-start.2
  2.6 0.0 copy-start.3
  2.6 14.0 %all_to_all.20 = f32[32,2,128]{2,1,0:T(2,128)S(1)} all-to-all(f32[32,2,128]{2,1,0:T(2,128)S(1)} %bitcast.25), channel_id=1, replica_groups=mesh['group'=1,'wide'=32] {'wide'}, dimensions={0} | all-to-all | bytes 65536 | tf_op jit(solution)/shard_map/all_to_all | solution.py:37
  16.6 0.0 collective-permute-done.refs_2_
  16.6 0.0 copy-done
  16.6 0.0 copy-done.1
  16.7 0.0 copy-done.2
  16.7 0.0 copy-done.3
  16.7 0.0 copy-start.4
  16.7 0.0 copy-start.5
  16.7 0.3 shard_map.147
  17.0 9.5 %all_to_all.21.parts_ref = bf16[32,3,4,128]{3,2,1,0:T(4,128)(2,1)S(1)} all-to-all(bf16[32,3,4,128]{3,2,1,0:T(4,128)(2,1)S(1)} %shard_map.147), channel_id=1, replica_groups=mesh['group'=1,'wide'=32] {'wide'}, dimensions={0} | all-to-all | bytes 196608 | tf_op jit(solution)/shard_map/all_to_all | solution.py:37
  26.5 0.0 copy-done.4
  26.5 0.0 copy-done.5
  26.5 0.2 shard_map.148
  26.7 9.5 %all_to_all.22.blocks_ref = bf16[32,3,4,128]{3,2,1,0:T(4,128)(2,1)S(1)} all-to-all(bf16[32,3,4,128]{3,2,1,0:T(4,128)(2,1)S(1)} %get-tuple-element.14), channel_id=1, replica_groups=mesh['group'=1,'wide'=32] {'wide'}, dimensions={0} | all-to-all | bytes 196608 | tf_op jit(solution)/shard_map/all_to_all | solution.py:37
  36.2 0.1 collective-permute-start.1
  36.3 1.1 %shard_map.149 = (f32[32,576]{1,0:T(8,128)S(1)}, f32[32,576]{1,0:T(8,128)S(1)}) custom-call(bf16[32,3,4,128]{3,2,1,0:T(4,128)(2,1)S(1)} %all_to_all.22.blocks_ref, bf16[576,3072]{1,0:T(8,128)(2,1)S(1)} %bitcast.12, bf16[576,3072]{1,0:T(8,128)(2,1)S(1)} %bitcast.17), custom_call_target="tpu_custom_call" | custom-call | flops 113246208 | bytes 7077888 | tf_op jit(solution)/shard_map/pallas_call | solution.py:343
  37.4 0.1 collective-permute-done.1.blocks_ref
  37.5 1.5 %shard_map.150 = (bf16[32,576]{1,0:T(8,128)(2,1)S(1)}, bf16[32,1536]{1,0:T(8,128)(2,1)S(1)}) custom-call(bf16[32,3,4,128]{3,2,1,0:T(4,128)(2,1)S(1)} %collective-permute-done.1.blocks_ref, bf16[576,3072]{1,0:T(8,128)(2,1)S(1)} %bitcast.13, bf16[576,3072]{1,0:T(8,128)(2,1)S(1)} %bitcast.18, bf16[576,3072]{1,0:T(8,128)(2,1)S(1)} %bitcast.22, ...), custom_call_target="tpu_custom_call" | custom-call | flops 169869312 | bytes 7077888 | tf_op jit(solution)/shard_map/pallas_call | solution.py:352
  39.0 0.4 collective-permute-start.2
  39.4 0.4 shard_map.151.own_ref
  39.8 0.6 %collective-permute-done.2.other_ref = bf16[32,1536]{1,0:T(8,128)(2,1)S(1)} collective-permute-done((bf16[32,1536]{1,0:T(8,128)(2,1)S(1)}, bf16[32,1536]{1,0:T(8,128)(2,1)S(1)}, u32[]{:S(2)}, u32[]{:S(2)}) %collective-permute-start.2) | collective-permute-done | bytes 98336 | tf_op jit(solution)/shard_map/ppermute | solution.py:52
  40.3 0.1 shard_map.152
  40.4 9.5 %all_to_all.23.parts_ref = bf16[32,3,4,128]{3,2,1,0:T(4,128)(2,1)S(1)} all-to-all(bf16[32,3,4,128]{3,2,1,0:T(4,128)(2,1)S(1)} %shard_map.152), channel_id=1, replica_groups=mesh['group'=1,'wide'=32] {'wide'}, dimensions={0} | all-to-all | bytes 196608 | tf_op jit(solution)/shard_map/all_to_all | solution.py:37
  49.9 0.7 %shard_map.153 = bf16[1,3072]{1,0:T(2,128)(2,1)} custom-call(bf16[32,3,4,128]{3,2,1,0:T(4,128)(2,1)S(1)} %all_to_all.23.parts_ref, f32[24,128]{1,0:T(8,128)S(1)} %get-tuple-element.20.hid_ref), custom_call_target="tpu_custom_call" | custom-call | flops 98304 | bytes 196608 | tf_op jit(solution)/shard_map/pallas_call | solution.py:374
  (1 shorter events, 0.0 us)
Async XLA Ops:
  0.0 16.6 %collective-permute-start = (bf16[128,3072]{1,0:T(8,128)(2,1)}, bf16[128,3072]{1,0:T(8,128)(2,1)S(1)}, u32[]{:S(2)}, u32[]{:S(2)}) collective-permute-start(bf16[128,3072]{1,0:T(8,128)(2,1)} %refs_1_.1), channel_id=1, source_target_pairs={{0,1},{1,0},{2,3},{3,2},{4,5},{5,4},{6,7},{7,6},{8,9},{9,8},{10,11... | collective-permute-start | bytes 2359304 | tf_op jit(solution)/shard_map/ppermute | solution.py:52
  2.6 14.1 %copy-start = (bf16[1,576,3072]{2,1,0:T(8,128)(2,1)S(1)}, bf16[1,576,3072]{2,1,0:T(8,128)(2,1)}, u32[]{:S(2)}) copy-start(bf16[1,576,3072]{2,1,0:T(8,128)(2,1)} %param.25) | copy-start | bytes 10616836
  2.6 14.1 %copy-start.1 = (bf16[1,576,3072]{2,1,0:T(8,128)(2,1)S(1)}, bf16[1,576,3072]{2,1,0:T(8,128)(2,1)}, u32[]{:S(2)}) copy-start(bf16[1,576,3072]{2,1,0:T(8,128)(2,1)} %param.26) | copy-start | bytes 10616836
  2.6 14.1 %copy-start.2 = (bf16[1,576,3072]{2,1,0:T(8,128)(2,1)S(1)}, bf16[1,576,3072]{2,1,0:T(8,128)(2,1)}, u32[]{:S(2)}) copy-start(bf16[1,576,3072]{2,1,0:T(8,128)(2,1)} %param.27) | copy-start | bytes 10616836
  2.6 14.1 %copy-start.3 = (bf16[128,3072]{1,0:T(8,128)(2,1)S(1)}, bf16[128,3072]{1,0:T(8,128)(2,1)}, u32[]{:S(2)}) copy-start(bf16[128,3072]{1,0:T(8,128)(2,1)} %refs_1_.1) | copy-start | bytes 2359300
  16.7 9.8 %copy-start.4 = (bf16[1,3072]{1,0:T(2,128)(2,1)S(1)}, bf16[1,3072]{1,0:T(2,128)(2,1)}, u32[]{:S(2)}) copy-start(bf16[1,3072]{1,0:T(2,128)(2,1)} %resid_ref.1) | copy-start | bytes 18436
  16.7 9.8 %copy-start.5 = (f32[3072]{0:T(1024)S(1)}, f32[3072]{0:T(1024)}, u32[]{:S(2)}) copy-start(f32[3072]{0:T(1024)} %param.24) | copy-start | bytes 36868
  36.2 1.3 %collective-permute-start.1 = (bf16[32,3,4,128]{3,2,1,0:T(4,128)(2,1)S(1)}, bf16[32,3,4,128]{3,2,1,0:T(4,128)(2,1)S(1)}, u32[]{:S(2)}, u32[]{:S(2)}) collective-permute-start(bf16[32,3,4,128]{3,2,1,0:T(4,128)(2,1)S(1)} %all_to_all.22.blocks_ref), channel_id=1, source_target_pairs={{0,1},{1,0},{2,3},{3,2},{4,5},{5,4},{6,7},{7,6},{8,9},{9,8},{10,11... | collective-permute-start | bytes 294920 | tf_op jit(solution)/shard_map/ppermute | solution.py:52
  39.0 1.4 %collective-permute-start.2 = (bf16[32,1536]{1,0:T(8,128)(2,1)S(1)}, bf16[32,1536]{1,0:T(8,128)(2,1)S(1)}, u32[]{:S(2)}, u32[]{:S(2)}) collective-permute-start(bf16[32,1536]{1,0:T(8,128)(2,1)S(1)} %get-tuple-element.19), channel_id=1, source_target_pairs={{0,1},{1,0},{2,3},{3,2},{4,5},{5,4},{6,7},{7,6},{8,9},{9,8},{10,11... | collective-permute-start | bytes 294920 | tf_op jit(solution)/shard_map/ppermute | solution.py:52
